TPU v7x, 512 devices: a whole 4x8x8 slice. The times are simulated.
512 devices in a mesh: rows: 32 (over z, x), seq: 16 (over y, core).
Axes of the slice: x: 4, y: 8, z: 8, core: 2. Of those that a mesh axis runs over, the one named last changes fastest.
Arguments:
- qkv: bfloat16 [32, 1024, 3840], P('rows', 'seq'), may hold values from -24 to 24
- hidden: bfloat16 [32, 1024, 1280], P('rows', 'seq'), may hold values from -3 to 3
- segment_ids: int32 [32, 1024], P('rows', 'seq'), may hold values from 0 to 4, as said below
- key_keep: int32 [32, 1024], P('rows', 'seq'), may hold values 0 or 1
- grid_sizes: int32 [32, 4, 2], P('rows'), may hold values from 8 to 16, as said below
- owner_slots: int32 [32, 4], P('rows'), may hold values from 0 to 15, as said below
- out_weight: bfloat16 [1280, 1280], P('rows'), may hold values from -0.15625 to 0.15625
- norm_gain: float32 [1280], replicated, may hold values from 0.5 to 1.5
- norm_bias: float32 [1280], replicated, may hold values from -1.5 to 1.5
- merge_weight: bfloat16 [5120, 4096], P(None, 'seq'), may hold values from -0.078125 to 0.078125
Outputs:
- normed: bfloat16 [32, 1024, 1280], P('rows', 'seq')
- request_norm: float32 [32, 16], P('rows', 'seq')
- request_peak: float32 [32, 16], P('rows', 'seq')
Inputs may be any that keep to these rules, and one draw needn't show every extreme that they name: `segment_ids`: segment ids never fall along a pack: image j covers h_j w_j tokens right after image j - 1, and tokens after the last image carry 4; every pack ends with some such padding. Inside an image each aligned group of 4 tokens is one 2 x 2 block of the patch grid, blocks in row-major order. `grid_sizes`: both sides are even; rows run from 8 to 16, columns from 8 to 14; the first image of every pack has 16 rows and 14 columns; the images of a pack agree with segment_ids. `owner_slots`: the images of one pack have distinct slots.
All inputs are finite; a program needn't handle non-finite values. No bound on the sum of `key_keep` on one device may be relied on, other than what follows from the above.
Results may differ from a plain program's by a relative error of at most 0.0057.
Values may be sent and summed in bfloat16 or wider, within the bound.
No kernel may reach another device: no remote copies, remote signals or barrier semaphores. Data moves between devices by JAX's collectives and lax.ppermute only.
A program may use at most 64 MiB of HBM per device.

v0:
```python
import jax
import jax.numpy as jnp
import numpy as np
from jax import lax
from jax.experimental import pallas as pl
from jax.experimental.pallas import tpu as pltpu
from jax.sharding import PartitionSpec as P


D = 1280
HEADS = 16
HD = 80
OUT = 4096
IMGS = 4
SEQ = 1024
TOK = 64
CHIPS = 8
MAXIMG = 896
NEG = -1e30


F32 = jnp.float32
BF16 = jnp.bfloat16
VM = pl.BlockSpec(memory_space=pltpu.VMEM)
SM = pl.BlockSpec(memory_space=pltpu.SMEM)


def iota(shape, dim):
    return lax.broadcasted_iota(jnp.int32, shape, dim)


def image_bounds(grid_ref):
    starts, ends, total = [], [], 0
    for j in range(IMGS):
        starts.append(total)
        total = total + grid_ref[0, 0, j] * grid_ref[0, 1, j]
        ends.append(total)
    return starts, ends


def rotary_kernel(grid_ref, keep_ref, qkv_ref, out_ref):
    starts, ends = image_bounds(grid_ref)
    place = lax.axis_index("seq") * TOK + iota((TOK, 256), 0)
    begin = jnp.zeros((TOK, 256), jnp.int32)
    width = jnp.full((TOK, 256), 2, jnp.int32)
    for j in range(IMGS):
        inside = (place >= starts[j]) & (place < ends[j])
        begin = jnp.where(inside, starts[j], begin)
        width = jnp.where(inside, grid_ref[0, 1, j], width)
    valid = place < ends[IMGS - 1]
    offset = place - begin
    square = lax.shift_right_logical(offset, 2)
    corner = offset & 3
    half = lax.shift_right_logical(width, 1)
    line = jnp.floor((square.astype(F32) + 0.5) / half.astype(F32)).astype(jnp.int32)
    row = 2 * line + lax.shift_right_logical(corner, 1)
    col = 2 * (square - line * half) + (corner & 1)
    row = jnp.where(valid, row, 0).astype(F32)
    col = jnp.where(valid, col, 0).astype(F32)
    lane = iota((TOK, 256), 1) & 127
    rotated = lane < HD
    pair = lane
    for _ in range(5):
        pair = jnp.where(pair >= 20, pair - 20, pair)
    rate = jnp.exp(pair.astype(F32) * (-np.log(10000.0) / 20))
    angle = jnp.where(lane < HD // 2, row, col) * rate
    cosine = jnp.where(rotated, jnp.cos(angle), 1.0)
    low = (lane < 20) | ((lane >= 40) & (lane < 60))
    sine = jnp.sin(angle)
    sine = jnp.where(rotated, jnp.where(low, -sine, sine), 0.0)
    diagonal = iota((TOK, TOK), 0) == iota((TOK, TOK), 1)
    flags = jnp.where(diagonal, keep_ref[...].astype(F32), 0.0)
    tail = jnp.broadcast_to(jnp.sum(flags, axis=1, keepdims=True), (TOK, 16))
    z = lax.shift_right_logical(lax.axis_index("rows"), 2)
    for head in range(HEADS):
        behind = (z - head // 2) & 7
        ahead = (head // 2 - z) & 7
        low_core = (behind >= 1) & (behind <= 4)
        place = jnp.where(low_core, behind - 1, (ahead + 3) & 3) + 4 * (head % 2)
        dest = 2 * place + jnp.where(low_core, 0, 1)
        q = qkv_ref[0, :, head * HD : head * HD + HD].astype(F32)
        k = qkv_ref[0, :, D + head * HD : D + head * HD + HD].astype(F32)
        v = qkv_ref[0, :, 2 * D + head * HD : 2 * D + head * HD + HD].astype(F32)
        full = jnp.concatenate([q, v[:, :48], k, v[:, 48:], tail], axis=1)
        swapped = jnp.where(low, pltpu.roll(full, 256 - 20, 1), pltpu.roll(full, 20, 1))
        out_ref[dest] = (full * cosine + swapped * sine).astype(BF16)


def attention_kernel(grid_ref, x_ref, out_ref):
    starts, ends = image_bounds(grid_ref)
    pick = jnp.where(iota((8, 128), 1) == 112, 1.0, 0.0).astype(BF16)
    keep = lax.dot_general(
        pick, x_ref[:, 128:], (((1,), (1,)), ((), ())), preferred_element_type=F32
    )[0:1]
    key_place = jnp.where(keep > 0.5, iota((1, SEQ), 1), -1)
    query_lane = iota((128, 128), 1) < HD

    def emit(chip, rows):
        flipped = jnp.transpose(rows)
        out_ref[chip, 0] = flipped[80:120].astype(BF16)
        out_ref[chip, 1] = jnp.concatenate(
            [flipped[120:128], flipped[208:240]], axis=0
        ).astype(BF16)

    for chip in range(MAXIMG // 128):
        first = chip * 128
        low = max(0, first - 256)
        high = min(MAXIMG, first + 384)
        query = jnp.where(query_lane, x_ref[first : first + 128, 0:128], 0)
        scores = lax.dot_general(
            query,
            x_ref[low:high, 128:256],
            (((1,), (1,)), ((), ())),
            preferred_element_type=F32,
        ) * HD ** (-0.5)
        place = first + iota((128, 1), 0)
        lo = place
        hi = place
        for j in range(IMGS):
            inside = (place >= starts[j]) & (place < ends[j])
            lo = jnp.where(inside, starts[j], lo)
            hi = jnp.where(inside, ends[j], hi)
        keys = key_place[:, low:high]
        same = (keys >= lo) & (keys < hi)
        own = iota((1, high - low), 1) + low == place
        scores = jnp.where(same | own, scores, NEG)
        top = jnp.max(scores, axis=1, keepdims=True)
        weights = jnp.exp(scores - top)
        total = jnp.sum(weights, axis=1, keepdims=True)
        summed = jnp.dot(
            weights.astype(BF16), x_ref[low:high, :], preferred_element_type=F32
        )
        emit(chip, summed / total)
    emit(CHIPS - 1, x_ref[MAXIMG:SEQ, :].astype(F32))


def mix_kernel(heads_ref, hidden_ref, own_ref, plus_ref, minus_ref, two_ref, out_ref):
    core = lax.axis_index("seq") & 1
    here = lax.axis_index("rows") & 3
    heads = []
    for step in (0, -1, 1, 2):
        x = (here + step) & 3
        upper, half = lax.shift_right_logical(x, 1), x & 1
        heads += [heads_ref[i + 4 * upper, half] for i in range(4)]
    weight = [ref[...] for ref in (own_ref, plus_ref, minus_ref, two_ref)]
    out_ref[...] = lax.dot_general(
        jnp.concatenate(heads, axis=0),
        jnp.concatenate(weight, axis=0),
        (((0,), (0,)), ((), ())),
        preferred_element_type=F32,
    )
    mine = pl.ds(pl.multiple_of(core * TOK, TOK), TOK)
    out_ref[mine, :] = out_ref[mine, :] + hidden_ref[0].astype(F32)


def norm_kernel(
    own_ref, recv_ref, gain_ref, bias_ref, normed_ref, first_ref, second_ref, keep_ref
):
    mixed = own_ref[...] + recv_ref[...]
    centred = mixed - jnp.mean(mixed, axis=1, keepdims=True)
    spread = jnp.mean(centred * centred, axis=1, keepdims=True)
    normed = centred * lax.rsqrt(spread + 1e-05) * gain_ref[...].reshape(1, D)
    normed = (normed + bias_ref[...].reshape(1, D)).astype(BF16)
    keep_ref[...] = normed
    core = lax.axis_index("seq") & 1
    normed_ref[0] = keep_ref[pl.ds(pl.multiple_of(core * TOK, TOK), TOK), :]
    line = iota((128, 128), 0)
    half = (lax.shift_right_logical(line, 6) + core) & 1
    source = TOK * half + 4 * (line & 15) + (lax.shift_right_logical(line, 4) & 3)
    order = jnp.where(iota((128, 128), 1) == source, 1.0, 0.0).astype(BF16)
    chunks = jnp.dot(order, normed, preferred_element_type=F32).astype(BF16)
    first_ref[...] = chunks[:TOK]
    second_ref[...] = chunks[TOK:]


def project_kernel(grid_ref, owner_ref, wa_ref, wb_ref, *refs):
    out_ref = refs[CHIPS]
    halves = []
    for w_ref in (wa_ref, wb_ref):
        part = 0.0
        for corner in range(4):
            rows = jnp.concatenate(
                [b[16 * corner : 16 * corner + 16, :] for b in refs[:CHIPS]], axis=0
            )
            part = part + jnp.dot(
                rows, w_ref[D * corner : D * corner + D, :], preferred_element_type=F32
            )
        halves.append(part)
    done = jnp.concatenate(halves, axis=1)
    squares = jnp.sum(done * done, axis=1, keepdims=True)
    peaks = jnp.max(done, axis=1, keepdims=True)
    _, ends = image_bounds(grid_ref)
    line = iota((128, 128), 0)
    index = lax.axis_index("seq")
    core = index & 1
    chunk = lax.shift_right_logical(line, 4)
    step = lax.shift_right_logical(chunk + 1, 1)
    second = ((chunk & 1) == 0) & (chunk > 0)
    half = jnp.where(second, 1 - core, core)
    step = jnp.where(core == 0, -step, step)
    source = (lax.shift_right_logical(index, 1) + step) & 7
    token = source * 128 + half * TOK + 4 * (line & 15)
    slot = jnp.full((128, 128), -1, jnp.int32)
    for j in reversed(range(IMGS)):
        slot = jnp.where(token < ends[j], owner_ref[0, j], slot)
    hot = slot == iota((128, 128), 1)
    sums = jnp.sum(jnp.where(hot, squares, 0.0), axis=0, keepdims=True)
    tops = jnp.max(jnp.where(hot, peaks, NEG), axis=0, keepdims=True)
    both = jnp.where(line == 0, sums, jnp.where(line == 1, tops, 0.0))
    out_ref[...] = jnp.transpose(both)[:16]


def final_kernel(grid_ref, owner_ref, stats_ref, norm_ref, peak_ref):
    stats = stats_ref[...]
    total = jnp.sum(stats, axis=0, keepdims=True)[:, 0:1]
    top = jnp.max(stats, axis=0, keepdims=True)[:, 1:2]
    me = lax.axis_index("seq")
    count = 0
    for j in range(IMGS):
        size = lax.shift_right_logical(grid_ref[0, 0, j] * grid_ref[0, 1, j], 2)
        count = count + jnp.where(owner_ref[0, j] == me, size, 0)
    counts = jnp.full((1, 1), count, jnp.int32)
    divisor = (jnp.maximum(counts, 1) * OUT).astype(F32)
    norm_ref[...] = jnp.where(counts > 0, jnp.sqrt(total / divisor + 1e-06), 0.0)
    peak_ref[...] = jnp.where(counts > 0, top, 0.0)


def call(kernel, out, specs, scratch=(), flops=0, bytes_accessed=0, mib=8):
    many = isinstance(out, (tuple, list))
    return pl.pallas_call(
        kernel,
        out_shape=out,
        in_specs=specs,
        out_specs=tuple([VM] * len(out)) if many else VM,
        scratch_shapes=scratch,
        cost_estimate=pl.CostEstimate(
            flops=flops, bytes_accessed=bytes_accessed, transcendentals=0
        ),
        compiler_params=pltpu.CompilerParams(vmem_limit_bytes=mib << 20),
    )


def shape(dims, dtype):
    return jax.ShapeDtypeStruct(dims, dtype)


def chip_shift(x, step, flip=0):
    pairs = []
    for s in range(2 * CHIPS):
        chip, core = s // 2, s % 2
        pairs.append((s, ((chip + step) % CHIPS) * 2 + (core ^ flip)))
    return lax.ppermute(x, "seq", pairs)


def two_way(axes, value, move, count, cores=(0, 1)):
    pairs = []
    for index in range(count):
        core = index & 1
        if core in cores:
            pairs.append((index, move(index, 1 - 2 * core)))
    return lax.ppermute(value, axes, pairs)


def gather_weight(weight):
    def move(index, step):
        row, place = index // 16, index % 16
        return (row + 4 * step) % 32 * 16 + place

    blocks, value = [], weight
    for k in range(1, 5):
        cores = (0, 1) if k < 4 else (0,)
        value = two_way(("rows", "seq"), value, move, 512, cores)
        blocks.append(value)
    core = lax.axis_index("seq") & 1
    blocks[3] = jnp.where(core == 0, blocks[3], weight)
    bundle = jnp.concatenate(blocks, axis=0)

    def shift_x(step):
        pairs = [(r, (r & ~3) + ((r + step) & 3)) for r in range(32)]
        return lax.ppermute(bundle, "rows", pairs)

    return [bundle, shift_x(1), shift_x(-1), shift_x(2)]


def body(
    qkv,
    hidden,
    segment_ids,
    key_keep,
    grid_sizes,
    owner_slots,
    out_weight,
    norm_gain,
    norm_bias,
    merge_weight,
):
    del segment_ids
    grid_sizes = jnp.transpose(grid_sizes, (0, 2, 1))
    weight = gather_weight(out_weight)
    packed = call(
        rotary_kernel,
        shape((HEADS, TOK, 256), BF16),
        [SM, VM, VM],
        flops=1 << 22,
        bytes_accessed=1 << 20,
        mib=56,
    )(grid_sizes, key_keep, qkv)
    heads_all = lax.all_to_all(packed, "seq", split_axis=0, concat_axis=0, tiled=True)
    merge_other = chip_shift(merge_weight, 0, 1)
    head_out = call(
        attention_kernel,
        shape((CHIPS, 2, HD // 2, 128), BF16),
        [SM, VM],
        flops=1 << 29,
        bytes_accessed=1 << 20,
    )(grid_sizes, heads_all.reshape(SEQ, 256))
    groups = [[2 * c + p for c in range(CHIPS)] for p in range(2)]
    attended = lax.all_to_all(
        head_out,
        "seq",
        split_axis=0,
        concat_axis=0,
        axis_index_groups=groups,
        tiled=True,
    )
    mixed = call(
        mix_kernel,
        shape((128, D), F32),
        [VM] * 6,
        flops=1 << 28,
        bytes_accessed=3 << 20,
    )(attended, hidden, *weight)
    recv = chip_shift(mixed, 0, 1)
    normed, first, second = call(
        norm_kernel,
        (shape((1, TOK, D), BF16), shape((TOK, D), BF16), shape((TOK, D), BF16)),
        [VM] * 4,
        scratch=[pltpu.VMEM((128, D), BF16)],
        flops=1 << 22,
        bytes_accessed=1 << 20,
    )(mixed, recv, norm_gain, norm_bias)

    def move(index, step):
        return (index + 2 * step) % 16

    chunks = [first]
    for k in range(1, 5):
        first = two_way("seq", first, move, 16)
        chunks.append(first)
        if k < 4:
            second = two_way("seq", second, move, 16)
            chunks.append(second)
    stats = call(
        project_kernel,
        shape((16, 128), F32),
        [SM, SM] + [VM] * (2 + CHIPS),
        flops=1 << 29,
        bytes_accessed=7 << 20,
        mib=16,
    )(grid_sizes, owner_slots, merge_weight, merge_other, *chunks)
    stats = lax.all_to_all(stats, "seq", split_axis=0, concat_axis=0, tiled=True)
    norm, peak = call(
        final_kernel, (shape((1, 1), F32), shape((1, 1), F32)), [SM, SM, VM]
    )(grid_sizes, owner_slots, stats)
    return (normed, norm, peak)


def solution(mesh):
    placed = (
        P("rows", "seq", None),
        P("rows", "seq", None),
        P("rows", "seq"),
        P("rows", "seq"),
        P("rows", None, None),
        P("rows", None),
        P("rows", None),
        P(),
        P(),
        P(None, "seq"),
    )

    return jax.shard_map(
        body,
        mesh=mesh,
        in_specs=placed,
        out_specs=(P("rows", "seq", None), P("rows", "seq"), P("rows", "seq")),
        check_vma=False,
    )
```

profile of v0, /device:TPU:1, one launch (start us, length us, event | category | flops | bytes accessed | tf_op | source)
XLA Modules:
  0.0 130.3 jit_solution(12195909598512819644)
XLA Ops:
  0.6 11.5 %collective-permute-start = (bf16[40,1280]{1,0:T(8,128)(2,1)}, bf16[40,1280]{1,0:T(8,128)(2,1)S(1)}, u32[]{:S(2)}, u32[]{:S(2)}) collective-permute-start(bf16[40,1280]{1,0:T(8,128)(2,1)} %param.15), channel_id=1, source_target_pairs={{0,64},{1,449},{2,66},{3,451},{4,68},{5,453},{6,70},{7,455},{8,72}... | collective-permute-start | bytes 307208 | tf_op jit(solution)/shard_map/ppermute | solution.py:261
  12.1 2.0 %collective-permute-done = bf16[40,1280]{1,0:T(8,128)(2,1)S(1)} collective-permute-done((bf16[40,1280]{1,0:T(8,128)(2,1)}, bf16[40,1280]{1,0:T(8,128)(2,1)S(1)}, u32[]{:S(2)}, u32[]{:S(2)}) %collective-permute-start) | collective-permute-done | bytes 102432 | tf_op jit(solution)/shard_map/ppermute | solution.py:261
  14.1 4.8 %collective-permute-start.1 = (bf16[40,1280]{1,0:T(8,128)(2,1)S(1)}, bf16[40,1280]{1,0:T(8,128)(2,1)S(1)}, u32[]{:S(2)}, u32[]{:S(2)}) collective-permute-start(bf16[40,1280]{1,0:T(8,128)(2,1)S(1)} %collective-permute-done), channel_id=1, source_target_pairs={{0,64},{1,449},{2,66},{3,451},{4,68},{5,453},{6,70},{7,455},{8,72}... | collective-permute-start | bytes 307208 | tf_op jit(solution)/shard_map/ppermute | solution.py:261
  19.0 3.8 %shard_map.112 = bf16[16,64,256]{2,1,0:T(8,128)(2,1)} custom-call(s32[1,2,4]{2,1,0:T(2,128)} %bitcast.9, s32[1,64]{1,0:T(1,128)} %keep_ref.1, bf16[1,64,3840]{2,1,0:T(8,128)(2,1)} %qkv_ref.1), custom_call_target="tpu_custom_call" | custom-call | flops 4194304 | bytes 1048576 | tf_op jit(solution)/shard_map/pallas_call | solution.py:300
  22.8 7.2 %all-to-all-start = ((bf16[16,64,256]{2,1,0:T(8,128)(2,1)}), bf16[16,64,256]{2,1,0:T(8,128)(2,1)S(1)}, u32[]{:S(2)}, u32[]{:S(2)}) async-start(bf16[16,64,256]{2,1,0:T(8,128)(2,1)} %shard_map.112), calls=%async_computation | async-start | bytes 1048576 | tf_op jit(solution)/shard_map/all_to_all | solution.py:308
  30.0 3.6 %collective-permute-start.2 = (bf16[40,1280]{1,0:T(8,128)(2,1)S(1)}, bf16[40,1280]{1,0:T(8,128)(2,1)S(1)}, u32[]{:S(2)}, u32[]{:S(2)}) collective-permute-start(bf16[40,1280]{1,0:T(8,128)(2,1)S(1)} %collective-permute-done.1), channel_id=1, source_target_pairs={{0,64},{1,449},{2,66},{3,451},{4,68},{5,453},{6,70},{7,455},{8,72}... | collective-permute-start | bytes 307208 | tf_op jit(solution)/shard_map/ppermute | solution.py:261
  33.6 1.9 %collective-permute-start.8 = (bf16[5120,256]{1,0:T(8,128)(2,1)}, bf16[5120,256]{1,0:T(8,128)(2,1)}, u32[]{:S(2)}, u32[]{:S(2)}) collective-permute-start(bf16[5120,256]{1,0:T(8,128)(2,1)} %wa_ref.1), channel_id=1, source_target_pairs={{0,1},{1,0},{2,3},{3,2},{4,5},{5,4},{6,7},{7,6},{8,9},{9,8},{10,11... | collective-permute-start | bytes 7864328 | tf_op jit(solution)/shard_map/ppermute | solution.py:252
  37.4 4.7 %collective-permute-start.6 = (bf16[160,1280]{1,0:T(8,128)(2,1)S(1)}, bf16[160,1280]{1,0:T(8,128)(2,1)}, u32[]{:S(2)}, u32[]{:S(2)}) collective-permute-start(bf16[160,1280]{1,0:T(8,128)(2,1)S(1)} %pad_maximum_fusion.own_ref), channel_id=1, source_target_pairs={{0,32},{16,48},{32,0},{48,16},{64,96},{80,112},{96,64},{112,80},{1... | collective-permute-start | bytes 1228808 | tf_op jit(solution)/shard_map/ppermute | solution.py:280
  42.0 2.8 %collective-permute-start.5 = (bf16[160,1280]{1,0:T(8,128)(2,1)S(1)}, bf16[160,1280]{1,0:T(8,128)(2,1)}, u32[]{:S(2)}, u32[]{:S(2)}) collective-permute-start(bf16[160,1280]{1,0:T(8,128)(2,1)S(1)} %pad_maximum_fusion.own_ref), channel_id=1, source_target_pairs={{0,48},{16,0},{32,16},{48,32},{64,112},{80,64},{96,80},{112,96},{1... | collective-permute-start | bytes 1228808 | tf_op jit(solution)/shard_map/ppermute | solution.py:280
  44.8 2.5 %collective-permute-start.4 = (bf16[160,1280]{1,0:T(8,128)(2,1)S(1)}, bf16[160,1280]{1,0:T(8,128)(2,1)}, u32[]{:S(2)}, u32[]{:S(2)}) collective-permute-start(bf16[160,1280]{1,0:T(8,128)(2,1)S(1)} %pad_maximum_fusion.own_ref), channel_id=1, source_target_pairs={{0,16},{16,32},{32,48},{48,0},{64,80},{80,96},{96,112},{112,64},{1... | collective-permute-start | bytes 1228808 | tf_op jit(solution)/shard_map/ppermute | solution.py:280
  47.3 3.1 %shard_map.113 = bf16[8,2,40,128]{3,2,1,0:T(8,128)(2,1)} custom-call(s32[1,2,4]{2,1,0:T(2,128)S(1)} %bitcast.10, bf16[1024,256]{1,0:T(8,128)(2,1)S(1)} %bitcast.6), custom_call_target="tpu_custom_call" | custom-call | flops 536870912 | bytes 1048576 | tf_op jit(solution)/shard_map/pallas_call | solution.py:310
  50.5 6.8 %all-to-all-start.1 = ((bf16[8,2,40,128]{3,2,1,0:T(8,128)(2,1)}), bf16[8,2,40,128]{3,2,1,0:T(8,128)(2,1)S(1)}, u32[]{:S(2)}, u32[]{:S(2)}) async-start(bf16[8,2,40,128]{3,2,1,0:T(8,128)(2,1)} %shard_map.113), calls=%async_computation.1 | async-start | bytes 327680 | tf_op jit(solution)/shard_map/all_to_all | solution.py:318
  57.3 1.9 %collective-permute-done.4.plus_ref = bf16[160,1280]{1,0:T(8,128)(2,1)} collective-permute-done((bf16[160,1280]{1,0:T(8,128)(2,1)S(1)}, bf16[160,1280]{1,0:T(8,128)(2,1)}, u32[]{:S(2)}, u32[]{:S(2)}) %collective-permute-start.4) | collective-permute-done | bytes 409632 | tf_op jit(solution)/shard_map/ppermute | solution.py:280
  59.2 6.3 %all-to-all-done.1.heads_ref = bf16[8,2,40,128]{3,2,1,0:T(8,128)(2,1)S(1)} async-done(((bf16[8,2,40,128]{3,2,1,0:T(8,128)(2,1)}), bf16[8,2,40,128]{3,2,1,0:T(8,128)(2,1)S(1)}, u32[]{:S(2)}, u32[]{:S(2)}) %all-to-all-start.1) | async-done | bytes 163872 | tf_op jit(solution)/shard_map/all_to_all | solution.py:318
  67.3 12.8 %collective-permute-start.7 = (f32[128,1280]{1,0:T(8,128)S(1)}, f32[128,1280]{1,0:T(8,128)S(1)}, u32[]{:S(2)}, u32[]{:S(2)}) collective-permute-start(f32[128,1280]{1,0:T(8,128)S(1)} %shard_map.114.own_ref), channel_id=1, source_target_pairs={{0,1},{1,0},{2,3},{3,2},{4,5},{5,4},{6,7},{7,6},{8,9},{9,8},{10,11... | collective-permute-start | bytes 1966088 | tf_op jit(solution)/shard_map/ppermute | solution.py:252
  84.8 2.2 %collective-permute-start.10 = (bf16[64,1280]{1,0:T(8,128)(2,1)S(1)}, bf16[64,1280]{1,0:T(8,128)(2,1)S(1)}, u32[]{:S(2)}, u32[]{:S(2)}) collective-permute-start(bf16[64,1280]{1,0:T(8,128)(2,1)S(1)} %get-tuple-element.10), channel_id=1, source_target_pairs={{0,2},{1,15},{2,4},{3,1},{4,6},{5,3},{6,8},{7,5},{8,10},{9,7},{10,... | collective-permute-start | bytes 491528 | tf_op jit(solution)/shard_map/ppermute | solution.py:261
  89.0 3.1 %collective-permute-start.11 = (bf16[64,1280]{1,0:T(8,128)(2,1)S(1)}, bf16[64,1280]{1,0:T(8,128)(2,1)S(1)}, u32[]{:S(2)}, u32[]{:S(2)}) collective-permute-start(bf16[64,1280]{1,0:T(8,128)(2,1)S(1)} %collective-permute-done.9.refs_1_), channel_id=1, source_target_pairs={{0,2},{1,15},{2,4},{3,1},{4,6},{5,3},{6,8},{7,5},{8,10},{9,7},{10,... | collective-permute-start | bytes 491528 | tf_op jit(solution)/shard_map/ppermute | solution.py:261
  92.1 2.2 %collective-permute-start.12 = (bf16[64,1280]{1,0:T(8,128)(2,1)S(1)}, bf16[64,1280]{1,0:T(8,128)(2,1)S(1)}, u32[]{:S(2)}, u32[]{:S(2)}) collective-permute-start(bf16[64,1280]{1,0:T(8,128)(2,1)S(1)} %collective-permute-done.10.refs_2_), channel_id=1, source_target_pairs={{0,2},{1,15},{2,4},{3,1},{4,6},{5,3},{6,8},{7,5},{8,10},{9,7},{10,... | collective-permute-start | bytes 491528 | tf_op jit(solution)/shard_map/ppermute | solution.py:261
  95.0 4.3 %collective-permute-start.13 = (bf16[64,1280]{1,0:T(8,128)(2,1)S(1)}, bf16[64,1280]{1,0:T(8,128)(2,1)S(1)}, u32[]{:S(2)}, u32[]{:S(2)}) collective-permute-start(bf16[64,1280]{1,0:T(8,128)(2,1)S(1)} %collective-permute-done.11.refs_3_), channel_id=1, source_target_pairs={{0,2},{1,15},{2,4},{3,1},{4,6},{5,3},{6,8},{7,5},{8,10},{9,7},{10,... | collective-permute-start | bytes 491528 | tf_op jit(solution)/shard_map/ppermute | solution.py:261
  99.4 2.2 %collective-permute-start.14 = (bf16[64,1280]{1,0:T(8,128)(2,1)S(1)}, bf16[64,1280]{1,0:T(8,128)(2,1)S(1)}, u32[]{:S(2)}, u32[]{:S(2)}) collective-permute-start(bf16[64,1280]{1,0:T(8,128)(2,1)S(1)} %collective-permute-done.12.refs_4_), channel_id=1, source_target_pairs={{0,2},{1,15},{2,4},{3,1},{4,6},{5,3},{6,8},{7,5},{8,10},{9,7},{10,... | collective-permute-start | bytes 491528 | tf_op jit(solution)/shard_map/ppermute | solution.py:261
  101.6 5.0 %collective-permute-start.15 = (bf16[64,1280]{1,0:T(8,128)(2,1)S(1)}, bf16[64,1280]{1,0:T(8,128)(2,1)S(1)}, u32[]{:S(2)}, u32[]{:S(2)}) collective-permute-start(bf16[64,1280]{1,0:T(8,128)(2,1)S(1)} %collective-permute-done.13.refs_5_), channel_id=1, source_target_pairs={{0,2},{1,15},{2,4},{3,1},{4,6},{5,3},{6,8},{7,5},{8,10},{9,7},{10,... | collective-permute-start | bytes 491528 | tf_op jit(solution)/shard_map/ppermute | solution.py:261
  106.6 2.2 %collective-permute-done.15.refs_7_ = bf16[64,1280]{1,0:T(8,128)(2,1)S(1)} collective-permute-done((bf16[64,1280]{1,0:T(8,128)(2,1)S(1)}, bf16[64,1280]{1,0:T(8,128)(2,1)S(1)}, u32[]{:S(2)}, u32[]{:S(2)}) %collective-permute-start.15) | collective-permute-done | bytes 163872 | tf_op jit(solution)/shard_map/ppermute | solution.py:261
  108.9 2.8 %shard_map.116 = f32[16,128]{1,0:T(8,128)S(1)} custom-call(s32[1,2,4]{2,1,0:T(2,128)S(1)} %bitcast.11, s32[1,4]{1,0:T(1,128)S(1)} %copy-done.5, bf16[5120,256]{1,0:T(8,128)(2,1)S(1)} %copy-done, bf16[5120,256]{1,0:T(8,128)(2,1)} %collective-permute-done.8.wb_ref, bf16[64,1280]{1,0:T(8,128)(2,1)S(1)} %get-tuple-element.9.refs_0_, ...), custom_call_target="tpu_custom_call" | custom-call | flops 536870912 | bytes 7340032 | tf_op jit(solution)/shard_map/pallas_call | solution.py:353
  111.6 17.5 %all_to_all.21 = f32[16,1,128]{2,1,0:T(1,128)S(1)} all-to-all(f32[16,1,128]{2,1,0:T(1,128)S(1)} %bitcast.7), channel_id=1, replica_groups=mesh['rows'=32,'seq'=16] {'seq'}, dimensions={0} | all-to-all | bytes 16384 | tf_op jit(solution)/shard_map/all_to_all | solution.py:361
  (33 shorter events, 11.9 us)
Async XLA Ops:
  0.6 46.7 %copy-start.2 = (s32[1,4,2]{1,2,0:T(2,128)S(1)}, s32[1,4,2]{1,2,0:T(2,128)}, u32[]{:S(2)}) copy-start(s32[1,4,2]{1,2,0:T(2,128)} %param.13) | copy-start | bytes 100
  0.6 13.5 %collective-permute-start = (bf16[40,1280]{1,0:T(8,128)(2,1)}, bf16[40,1280]{1,0:T(8,128)(2,1)S(1)}, u32[]{:S(2)}, u32[]{:S(2)}) collective-permute-start(bf16[40,1280]{1,0:T(8,128)(2,1)} %param.15), channel_id=1, source_target_pairs={{0,64},{1,449},{2,66},{3,451},{4,68},{5,453},{6,70},{7,455},{8,72}... | collective-permute-start | bytes 307208 | tf_op jit(solution)/shard_map/ppermute | solution.py:261
  14.1 15.9 %collective-permute-start.1 = (bf16[40,1280]{1,0:T(8,128)(2,1)S(1)}, bf16[40,1280]{1,0:T(8,128)(2,1)S(1)}, u32[]{:S(2)}, u32[]{:S(2)}) collective-permute-start(bf16[40,1280]{1,0:T(8,128)(2,1)S(1)} %collective-permute-done), channel_id=1, source_target_pairs={{0,64},{1,449},{2,66},{3,451},{4,68},{5,453},{6,70},{7,455},{8,72}... | collective-permute-start | bytes 307208 | tf_op jit(solution)/shard_map/ppermute | solution.py:261
  19.0 46.6 %copy-start.1 = (bf16[1,64,1280]{2,1,0:T(8,128)(2,1)S(1)}, bf16[1,64,1280]{2,1,0:T(8,128)(2,1)}, u32[]{:S(2)}) copy-start(bf16[1,64,1280]{2,1,0:T(8,128)(2,1)} %hidden_ref.1) | copy-start | bytes 491524
  22.8 24.6 %all-to-all-start = ((bf16[16,64,256]{2,1,0:T(8,128)(2,1)}), bf16[16,64,256]{2,1,0:T(8,128)(2,1)S(1)}, u32[]{:S(2)}, u32[]{:S(2)}) async-start(bf16[16,64,256]{2,1,0:T(8,128)(2,1)} %shard_map.112), calls=%async_computation | async-start | bytes 1048576 | tf_op jit(solution)/shard_map/all_to_all | solution.py:308
  30.0 5.7 %collective-permute-start.2 = (bf16[40,1280]{1,0:T(8,128)(2,1)S(1)}, bf16[40,1280]{1,0:T(8,128)(2,1)S(1)}, u32[]{:S(2)}, u32[]{:S(2)}) collective-permute-start(bf16[40,1280]{1,0:T(8,128)(2,1)S(1)} %collective-permute-done.1), channel_id=1, source_target_pairs={{0,64},{1,449},{2,66},{3,451},{4,68},{5,453},{6,70},{7,455},{8,72}... | collective-permute-start | bytes 307208 | tf_op jit(solution)/shard_map/ppermute | solution.py:261
  33.6 75.2 %collective-permute-start.8 = (bf16[5120,256]{1,0:T(8,128)(2,1)}, bf16[5120,256]{1,0:T(8,128)(2,1)}, u32[]{:S(2)}, u32[]{:S(2)}) collective-permute-start(bf16[5120,256]{1,0:T(8,128)(2,1)} %wa_ref.1), channel_id=1, source_target_pairs={{0,1},{1,0},{2,3},{3,2},{4,5},{5,4},{6,7},{7,6},{8,9},{9,8},{10,11... | collective-permute-start | bytes 7864328 | tf_op jit(solution)/shard_map/ppermute | solution.py:252
  35.7 0.7 collective-permute-start.3
  37.3 44.5 %copy-start.3 = (f32[1280]{0:T(1024)S(1)}, f32[1280]{0:T(1024)}, u32[]{:S(2)}) copy-start(f32[1280]{0:T(1024)} %gain_ref.1) | copy-start | bytes 15364
  37.4 44.5 %copy-start.4 = (f32[1280]{0:T(1024)S(1)}, f32[1280]{0:T(1024)}, u32[]{:S(2)}) copy-start(f32[1280]{0:T(1024)} %bias_ref.1) | copy-start | bytes 15364
  37.4 19.9 %collective-permute-start.6 = (bf16[160,1280]{1,0:T(8,128)(2,1)S(1)}, bf16[160,1280]{1,0:T(8,128)(2,1)}, u32[]{:S(2)}, u32[]{:S(2)}) collective-permute-start(bf16[160,1280]{1,0:T(8,128)(2,1)S(1)} %pad_maximum_fusion.own_ref), channel_id=1, source_target_pairs={{0,32},{16,48},{32,0},{48,16},{64,96},{80,112},{96,64},{112,80},{1... | collective-permute-start | bytes 1228808 | tf_op jit(solution)/shard_map/ppermute | solution.py:280
  42.0 15.2 %collective-permute-start.5 = (bf16[160,1280]{1,0:T(8,128)(2,1)S(1)}, bf16[160,1280]{1,0:T(8,128)(2,1)}, u32[]{:S(2)}, u32[]{:S(2)}) collective-permute-start(bf16[160,1280]{1,0:T(8,128)(2,1)S(1)} %pad_maximum_fusion.own_ref), channel_id=1, source_target_pairs={{0,48},{16,0},{32,16},{48,32},{64,112},{80,64},{96,80},{112,96},{1... | collective-permute-start | bytes 1228808 | tf_op jit(solution)/shard_map/ppermute | solution.py:280
  44.8 14.4 %collective-permute-start.4 = (bf16[160,1280]{1,0:T(8,128)(2,1)S(1)}, bf16[160,1280]{1,0:T(8,128)(2,1)}, u32[]{:S(2)}, u32[]{:S(2)}) collective-permute-start(bf16[160,1280]{1,0:T(8,128)(2,1)S(1)} %pad_maximum_fusion.own_ref), channel_id=1, source_target_pairs={{0,16},{16,32},{32,48},{48,0},{64,80},{80,96},{96,112},{112,64},{1... | collective-permute-start | bytes 1228808 | tf_op jit(solution)/shard_map/ppermute | solution.py:280
  50.5 58.4 %copy-start = (bf16[5120,256]{1,0:T(8,128)(2,1)S(1)}, bf16[5120,256]{1,0:T(8,128)(2,1)}, u32[]{:S(2)}) copy-start(bf16[5120,256]{1,0:T(8,128)(2,1)} %wa_ref.1) | copy-start | bytes 7864324
  50.5 58.4 %copy-start.5 = (s32[1,4]{1,0:T(1,128)S(1)}, s32[1,4]{1,0:T(1,128)}, u32[]{:S(2)}) copy-start(s32[1,4]{1,0:T(1,128)} %owner_ref.3) | copy-start | bytes 52
  50.5 15.1 %all-to-all-start.1 = ((bf16[8,2,40,128]{3,2,1,0:T(8,128)(2,1)}), bf16[8,2,40,128]{3,2,1,0:T(8,128)(2,1)S(1)}, u32[]{:S(2)}, u32[]{:S(2)}) async-start(bf16[8,2,40,128]{3,2,1,0:T(8,128)(2,1)} %shard_map.113), calls=%async_computation.1 | async-start | bytes 327680 | tf_op jit(solution)/shard_map/all_to_all | solution.py:318
  67.3 14.5 %collective-permute-start.7 = (f32[128,1280]{1,0:T(8,128)S(1)}, f32[128,1280]{1,0:T(8,128)S(1)}, u32[]{:S(2)}, u32[]{:S(2)}) collective-permute-start(f32[128,1280]{1,0:T(8,128)S(1)} %shard_map.114.own_ref), channel_id=1, source_target_pairs={{0,1},{1,0},{2,3},{3,2},{4,5},{5,4},{6,7},{7,6},{8,9},{9,8},{10,11... | collective-permute-start | bytes 1966088 | tf_op jit(solution)/shard_map/ppermute | solution.py:252
  82.9 6.1 %collective-permute-start.9 = (bf16[64,1280]{1,0:T(8,128)(2,1)S(1)}, bf16[64,1280]{1,0:T(8,128)(2,1)S(1)}, u32[]{:S(2)}, u32[]{:S(2)}) collective-permute-start(bf16[64,1280]{1,0:T(8,128)(2,1)S(1)} %get-tuple-element.9.refs_0_), channel_id=1, source_target_pairs={{0,2},{1,15},{2,4},{3,1},{4,6},{5,3},{6,8},{7,5},{8,10},{9,7},{10,... | collective-permute-start | bytes 491528 | tf_op jit(solution)/shard_map/ppermute | solution.py:261
  84.8 7.3 %collective-permute-start.10 = (bf16[64,1280]{1,0:T(8,128)(2,1)S(1)}, bf16[64,1280]{1,0:T(8,128)(2,1)S(1)}, u32[]{:S(2)}, u32[]{:S(2)}) collective-permute-start(bf16[64,1280]{1,0:T(8,128)(2,1)S(1)} %get-tuple-element.10), channel_id=1, source_target_pairs={{0,2},{1,15},{2,4},{3,1},{4,6},{5,3},{6,8},{7,5},{8,10},{9,7},{10,... | collective-permute-start | bytes 491528 | tf_op jit(solution)/shard_map/ppermute | solution.py:261
  89.0 6.1 %collective-permute-start.11 = (bf16[64,1280]{1,0:T(8,128)(2,1)S(1)}, bf16[64,1280]{1,0:T(8,128)(2,1)S(1)}, u32[]{:S(2)}, u32[]{:S(2)}) collective-permute-start(bf16[64,1280]{1,0:T(8,128)(2,1)S(1)} %collective-permute-done.9.refs_1_), channel_id=1, source_target_pairs={{0,2},{1,15},{2,4},{3,1},{4,6},{5,3},{6,8},{7,5},{8,10},{9,7},{10,... | collective-permute-start | bytes 491528 | tf_op jit(solution)/shard_map/ppermute | solution.py:261
  92.1 7.3 %collective-permute-start.12 = (bf16[64,1280]{1,0:T(8,128)(2,1)S(1)}, bf16[64,1280]{1,0:T(8,128)(2,1)S(1)}, u32[]{:S(2)}, u32[]{:S(2)}) collective-permute-start(bf16[64,1280]{1,0:T(8,128)(2,1)S(1)} %collective-permute-done.10.refs_2_), channel_id=1, source_target_pairs={{0,2},{1,15},{2,4},{3,1},{4,6},{5,3},{6,8},{7,5},{8,10},{9,7},{10,... | collective-permute-start | bytes 491528 | tf_op jit(solution)/shard_map/ppermute | solution.py:261
  95.0 6.6 %collective-permute-start.13 = (bf16[64,1280]{1,0:T(8,128)(2,1)S(1)}, bf16[64,1280]{1,0:T(8,128)(2,1)S(1)}, u32[]{:S(2)}, u32[]{:S(2)}) collective-permute-start(bf16[64,1280]{1,0:T(8,128)(2,1)S(1)} %collective-permute-done.11.refs_3_), channel_id=1, source_target_pairs={{0,2},{1,15},{2,4},{3,1},{4,6},{5,3},{6,8},{7,5},{8,10},{9,7},{10,... | collective-permute-start | bytes 491528 | tf_op jit(solution)/shard_map/ppermute | solution.py:261
  99.4 7.3 %collective-permute-start.14 = (bf16[64,1280]{1,0:T(8,128)(2,1)S(1)}, bf16[64,1280]{1,0:T(8,128)(2,1)S(1)}, u32[]{:S(2)}, u32[]{:S(2)}) collective-permute-start(bf16[64,1280]{1,0:T(8,128)(2,1)S(1)} %collective-permute-done.12.refs_4_), channel_id=1, source_target_pairs={{0,2},{1,15},{2,4},{3,1},{4,6},{5,3},{6,8},{7,5},{8,10},{9,7},{10,... | collective-permute-start | bytes 491528 | tf_op jit(solution)/shard_map/ppermute | solution.py:261
  101.6 7.2 %collective-permute-start.15 = (bf16[64,1280]{1,0:T(8,128)(2,1)S(1)}, bf16[64,1280]{1,0:T(8,128)(2,1)S(1)}, u32[]{:S(2)}, u32[]{:S(2)}) collective-permute-start(bf16[64,1280]{1,0:T(8,128)(2,1)S(1)} %collective-permute-done.13.refs_5_), channel_id=1, source_target_pairs={{0,2},{1,15},{2,4},{3,1},{4,6},{5,3},{6,8},{7,5},{8,10},{9,7},{10,... | collective-permute-start | bytes 491528 | tf_op jit(solution)/shard_map/ppermute | solution.py:261
where the time goes:
time: 131 us; the launch traced here: 130 us
  starting transfers between devices  80.4 us (61%)
  blocking collectives  17.5 us (13%)
  waiting for transfers between devices  16.9 us (13%)
  Pallas kernels  13.7 us (10%)
    ppermute x11, starting transfers between devices, two_way(): return lax.ppermute(value, axes, pairs)  41.7 us
    all_to_all x1, blocking collectives, body(): lax.all_to_all(stats, 'seq', split_axis=0, concat_axis=0, tiled=True)  17.5 us
    ppermute x2, starting transfers between devices, chip_shift(): return lax.ppermute(x, 'seq', pairs)  14.7 us
    ppermute x3, starting transfers between devices, shift_x(): return lax.ppermute(bundle, 'rows', pairs)  9.94 us
    all_to_all x1, starting transfers between devices, body(): lax.all_to_all(packed, 'seq', split_axis=0, concat_axis=0, tiled=True)  7.23 us
    ppermute x11, waiting for transfers between devices, two_way(): return lax.ppermute(value, axes, pairs)  6.92 us
    all_to_all x1, starting transfers between devices, body(): lax.all_to_all(head_out, 'seq', split_axis=0, concat_axis=0, axis_index_g...  6.8 us
    all_to_all x1, waiting for transfers between devices, body(): lax.all_to_all(head_out, 'seq', split_axis=0, concat_axis=0, axis_index_g...  6.34 us
  transfers between devices with their start and end apart: 18, of which 8 were waited for; matrix products, arithmetic and copies ran while one was open for 1% of the time, Pallas kernels for 7%

commit v1 on v0

--- a/solution.py
+++ b/solution.py
@@ -252,12 +252,12 @@
     return lax.ppermute(x, "seq", pairs)
 
 
-def two_way(axes, value, move, count, cores=(0, 1)):
+def two_way(axes, value, move, count, places, cores=(0, 1)):
     pairs = []
     for index in range(count):
         core = index & 1
         if core in cores:
-            pairs.append((index, move(index, 1 - 2 * core)))
+            pairs.append((index, move(index, places * (1 - 2 * core))))
     return lax.ppermute(value, axes, pairs)
 
 
@@ -266,11 +266,10 @@
         row, place = index // 16, index % 16
         return (row + 4 * step) % 32 * 16 + place
 
-    blocks, value = [], weight
+    blocks = []
     for k in range(1, 5):
         cores = (0, 1) if k < 4 else (0,)
-        value = two_way(("rows", "seq"), value, move, 512, cores)
-        blocks.append(value)
+        blocks.append(two_way(("rows", "seq"), weight, move, 512, k, cores))
     core = lax.axis_index("seq") & 1
     blocks[3] = jnp.where(core == 0, blocks[3], weight)
     bundle = jnp.concatenate(blocks, axis=0)
@@ -343,13 +342,14 @@
     def move(index, step):
         return (index + 2 * step) % 16
 
-    chunks = [first]
-    for k in range(1, 5):
-        first = two_way("seq", first, move, 16)
-        chunks.append(first)
-        if k < 4:
-            second = two_way("seq", second, move, 16)
-            chunks.append(second)
+    def send(value, places):
+        return two_way("seq", value, move, 16, places)
+
+    first1, second1 = send(first, 1), send(second, 1)
+    first2, second2 = send(first, 2), send(second, 2)
+    first3, second3 = send(first1, 2), send(second1, 2)
+    first4 = send(first2, 2)
+    chunks = [first, first1, second1, first2, second2, first3, second3, first4]
     stats = call(
         project_kernel,
         shape((16, 128), F32),

time: 131 us -> 125 us (0.954)
  starting transfers between devices: 80.4 us -> 72.5 us
  waiting for transfers between devices: 16.9 us -> 22.9 us
  blocking collectives: 17.5 us -> 13.7 us
    ppermute x11, starting transfers between devices: 41.7 us -> 34 us  [two_way(): return lax.ppermute(value, axes, pairs)]
    ppermute x11, waiting for transfers between devices: 6.92 us -> 13 us  [two_way(): return lax.ppermute(value, axes, pairs)]
    all_to_all x1, blocking collectives: 17.5 us -> 13.7 us  [body(): lax.all_to_all(stats, 'seq', split_axis=0, concat_axis=0, tiled=True)]
    all_to_all x1, starting transfers between devices: 7.23 us -> 3.47 us  [body(): lax.all_to_all(packed, 'seq', split_axis=0, concat_axis=0, tiled=True)]
    ppermute x2, starting transfers between devices: 14.7 us -> 18.2 us  [chip_shift(): return lax.ppermute(x, 'seq', pairs)]
  transfers between devices with their start and end apart: 18 -> 18, of which waited for: 8 -> 10; matrix products, arithmetic and copies ran while one was open for 1% -> 1% of each run, Pallas kernels for 7% -> 8%
where the time goes in v1:
time: 125 us
  starting transfers between devices  72.5 us (58%)
  waiting for transfers between devices  22.9 us (18%)
  blocking collectives  13.7 us (11%)
  Pallas kernels  13.6 us (11%)
    ppermute x11, starting transfers between devices, two_way(): return lax.ppermute(value, axes, pairs)  34 us
    ppermute x2, starting transfers between devices, chip_shift(): return lax.ppermute(x, 'seq', pairs)  18.2 us
    all_to_all x1, blocking collectives, body(): lax.all_to_all(stats, 'seq', split_axis=0, concat_axis=0, tiled=True)  13.7 us
    ppermute x11, waiting for transfers between devices, two_way(): return lax.ppermute(value, axes, pairs)  13 us
    ppermute x3, starting transfers between devices, shift_x(): return lax.ppermute(bundle, 'rows', pairs)  9.94 us
    all_to_all x1, starting transfers between devices, body(): lax.all_to_all(head_out, 'seq', split_axis=0, concat_axis=0, axis_index_g...  6.91 us
    all_to_all x1, waiting for transfers between devices, body(): lax.all_to_all(head_out, 'seq', split_axis=0, concat_axis=0, axis_index_g...  5.66 us
    pallas_call x1, Pallas kernels, body(): call(rotary_kernel, shape((HEADS, TOK, 256), BF16), [SM, VM, VM], flops=1...  3.81 us
  transfers between devices with their start and end apart: 18, of which 10 were waited for; matrix products, arithmetic and copies ran while one was open for 1% of the time, Pallas kernels for 8%

profile of v1, /device:TPU:1, one launch (start us, length us, event | category | flops | bytes accessed | tf_op | source)
XLA Modules:
  0.0 124.6 jit_solution(17966882600580596694)
XLA Ops:
  0.6 8.8 %collective-permute-start.8 = (bf16[5120,256]{1,0:T(8,128)(2,1)}, bf16[5120,256]{1,0:T(8,128)(2,1)}, u32[]{:S(2)}, u32[]{:S(2)}) collective-permute-start(bf16[5120,256]{1,0:T(8,128)(2,1)} %wa_ref.1), channel_id=1, source_target_pairs={{0,1},{1,0},{2,3},{3,2},{4,5},{5,4},{6,7},{7,6},{8,9},{9,8},{10,11... | collective-permute-start | bytes 7864328 | tf_op jit(solution)/shard_map/ppermute | solution.py:252
  9.4 3.8 %shard_map.112 = bf16[16,64,256]{2,1,0:T(8,128)(2,1)} custom-call(s32[1,2,4]{2,1,0:T(2,128)} %bitcast.9, s32[1,64]{1,0:T(1,128)} %keep_ref.1, bf16[1,64,3840]{2,1,0:T(8,128)(2,1)} %qkv_ref.1), custom_call_target="tpu_custom_call" | custom-call | flops 4194304 | bytes 1048576 | tf_op jit(solution)/shard_map/pallas_call | solution.py:299
  13.2 3.5 %all-to-all-start = ((bf16[16,64,256]{2,1,0:T(8,128)(2,1)}), bf16[16,64,256]{2,1,0:T(8,128)(2,1)S(1)}, u32[]{:S(2)}, u32[]{:S(2)}) async-start(bf16[16,64,256]{2,1,0:T(8,128)(2,1)} %shard_map.112), calls=%async_computation | async-start | bytes 1048576 | tf_op jit(solution)/shard_map/all_to_all | solution.py:307
  17.4 9.0 %collective-permute-start.2 = (bf16[40,1280]{1,0:T(8,128)(2,1)}, bf16[40,1280]{1,0:T(8,128)(2,1)S(1)}, u32[]{:S(2)}, u32[]{:S(2)}) collective-permute-start(bf16[40,1280]{1,0:T(8,128)(2,1)} %param.15), channel_id=1, source_target_pairs={{0,192},{1,321},{2,194},{3,323},{4,196},{5,325},{6,198},{7,327},{8... | collective-permute-start | bytes 307208 | tf_op jit(solution)/shard_map/ppermute | solution.py:261
  28.4 2.2 %collective-permute-start = (bf16[40,1280]{1,0:T(8,128)(2,1)}, bf16[40,1280]{1,0:T(8,128)(2,1)S(1)}, u32[]{:S(2)}, u32[]{:S(2)}) collective-permute-start(bf16[40,1280]{1,0:T(8,128)(2,1)} %param.15), channel_id=1, source_target_pairs={{0,64},{1,449},{2,66},{3,451},{4,68},{5,453},{6,70},{7,455},{8,72}... | collective-permute-start | bytes 307208 | tf_op jit(solution)/shard_map/ppermute | solution.py:261
  32.0 3.1 %collective-permute-done.1 = bf16[40,1280]{1,0:T(8,128)(2,1)S(1)} collective-permute-done((bf16[40,1280]{1,0:T(8,128)(2,1)}, bf16[40,1280]{1,0:T(8,128)(2,1)S(1)}, u32[]{:S(2)}, u32[]{:S(2)}) %collective-permute-start.1) | collective-permute-done | bytes 102432 | tf_op jit(solution)/shard_map/ppermute | solution.py:261
  36.4 4.7 %collective-permute-start.6 = (bf16[160,1280]{1,0:T(8,128)(2,1)S(1)}, bf16[160,1280]{1,0:T(8,128)(2,1)}, u32[]{:S(2)}, u32[]{:S(2)}) collective-permute-start(bf16[160,1280]{1,0:T(8,128)(2,1)S(1)} %pad_maximum_fusion.own_ref), channel_id=1, source_target_pairs={{0,32},{16,48},{32,0},{48,16},{64,96},{80,112},{96,64},{112,80},{1... | collective-permute-start | bytes 1228808 | tf_op jit(solution)/shard_map/ppermute | solution.py:279
  41.1 2.8 %collective-permute-start.5 = (bf16[160,1280]{1,0:T(8,128)(2,1)S(1)}, bf16[160,1280]{1,0:T(8,128)(2,1)}, u32[]{:S(2)}, u32[]{:S(2)}) collective-permute-start(bf16[160,1280]{1,0:T(8,128)(2,1)S(1)} %pad_maximum_fusion.own_ref), channel_id=1, source_target_pairs={{0,48},{16,0},{32,16},{48,32},{64,112},{80,64},{96,80},{112,96},{1... | collective-permute-start | bytes 1228808 | tf_op jit(solution)/shard_map/ppermute | solution.py:279
  43.9 2.5 %collective-permute-start.4 = (bf16[160,1280]{1,0:T(8,128)(2,1)S(1)}, bf16[160,1280]{1,0:T(8,128)(2,1)}, u32[]{:S(2)}, u32[]{:S(2)}) collective-permute-start(bf16[160,1280]{1,0:T(8,128)(2,1)S(1)} %pad_maximum_fusion.own_ref), channel_id=1, source_target_pairs={{0,16},{16,32},{32,48},{48,0},{64,80},{80,96},{96,112},{112,64},{1... | collective-permute-start | bytes 1228808 | tf_op jit(solution)/shard_map/ppermute | solution.py:279
  46.4 3.1 %shard_map.113 = bf16[8,2,40,128]{3,2,1,0:T(8,128)(2,1)} custom-call(s32[1,2,4]{2,1,0:T(2,128)S(1)} %bitcast.10, bf16[1024,256]{1,0:T(8,128)(2,1)S(1)} %bitcast.6), custom_call_target="tpu_custom_call" | custom-call | flops 536870912 | bytes 1048576 | tf_op jit(solution)/shard_map/pallas_call | solution.py:309
  49.5 6.9 %all-to-all-start.1 = ((bf16[8,2,40,128]{3,2,1,0:T(8,128)(2,1)}), bf16[8,2,40,128]{3,2,1,0:T(8,128)(2,1)S(1)}, u32[]{:S(2)}, u32[]{:S(2)}) async-start(bf16[8,2,40,128]{3,2,1,0:T(8,128)(2,1)} %shard_map.113), calls=%async_computation.1 | async-start | bytes 327680 | tf_op jit(solution)/shard_map/all_to_all | solution.py:317
  56.5 2.5 %collective-permute-done.4.plus_ref = bf16[160,1280]{1,0:T(8,128)(2,1)} collective-permute-done((bf16[160,1280]{1,0:T(8,128)(2,1)S(1)}, bf16[160,1280]{1,0:T(8,128)(2,1)}, u32[]{:S(2)}, u32[]{:S(2)}) %collective-permute-start.4) | collective-permute-done | bytes 409632 | tf_op jit(solution)/shard_map/ppermute | solution.py:279
  59.0 5.7 %all-to-all-done.1.heads_ref = bf16[8,2,40,128]{3,2,1,0:T(8,128)(2,1)S(1)} async-done(((bf16[8,2,40,128]{3,2,1,0:T(8,128)(2,1)}), bf16[8,2,40,128]{3,2,1,0:T(8,128)(2,1)S(1)}, u32[]{:S(2)}, u32[]{:S(2)}) %all-to-all-start.1) | async-done | bytes 163872 | tf_op jit(solution)/shard_map/all_to_all | solution.py:317
  66.4 9.4 %collective-permute-start.7 = (f32[128,1280]{1,0:T(8,128)S(1)}, f32[128,1280]{1,0:T(8,128)S(1)}, u32[]{:S(2)}, u32[]{:S(2)}) collective-permute-start(f32[128,1280]{1,0:T(8,128)S(1)} %shard_map.114.own_ref), channel_id=1, source_target_pairs={{0,1},{1,0},{2,3},{3,2},{4,5},{5,4},{6,7},{7,6},{8,9},{9,8},{10,11... | collective-permute-start | bytes 1966088 | tf_op jit(solution)/shard_map/ppermute | solution.py:252
  80.6 2.0 %collective-permute-start.11 = (bf16[64,1280]{1,0:T(8,128)(2,1)S(1)}, bf16[64,1280]{1,0:T(8,128)(2,1)S(1)}, u32[]{:S(2)}, u32[]{:S(2)}) collective-permute-start(bf16[64,1280]{1,0:T(8,128)(2,1)S(1)} %get-tuple-element.9.refs_0_), channel_id=1, source_target_pairs={{0,4},{1,13},{2,6},{3,15},{4,8},{5,1},{6,10},{7,3},{8,12},{9,5},{1... | collective-permute-start | bytes 491528 | tf_op jit(solution)/shard_map/ppermute | solution.py:261
  82.6 2.6 %collective-permute-start.9 = (bf16[64,1280]{1,0:T(8,128)(2,1)S(1)}, bf16[64,1280]{1,0:T(8,128)(2,1)S(1)}, u32[]{:S(2)}, u32[]{:S(2)}) collective-permute-start(bf16[64,1280]{1,0:T(8,128)(2,1)S(1)} %get-tuple-element.9.refs_0_), channel_id=1, source_target_pairs={{0,2},{1,15},{2,4},{3,1},{4,6},{5,3},{6,8},{7,5},{8,10},{9,7},{10,... | collective-permute-start | bytes 491528 | tf_op jit(solution)/shard_map/ppermute | solution.py:261
  85.2 5.0 %collective-permute-start.12 = (bf16[64,1280]{1,0:T(8,128)(2,1)S(1)}, bf16[64,1280]{1,0:T(8,128)(2,1)S(1)}, u32[]{:S(2)}, u32[]{:S(2)}) collective-permute-start(bf16[64,1280]{1,0:T(8,128)(2,1)S(1)} %get-tuple-element.10), channel_id=1, source_target_pairs={{0,4},{1,13},{2,6},{3,15},{4,8},{5,1},{6,10},{7,3},{8,12},{9,5},{1... | collective-permute-start | bytes 491528 | tf_op jit(solution)/shard_map/ppermute | solution.py:261
  90.2 4.2 %collective-permute-start.14 = (bf16[64,1280]{1,0:T(8,128)(2,1)S(1)}, bf16[64,1280]{1,0:T(8,128)(2,1)S(1)}, u32[]{:S(2)}, u32[]{:S(2)}) collective-permute-start(bf16[64,1280]{1,0:T(8,128)(2,1)S(1)} %collective-permute-done.10.refs_2_), channel_id=1, source_target_pairs={{0,4},{1,13},{2,6},{3,15},{4,8},{5,1},{6,10},{7,3},{8,12},{9,5},{1... | collective-permute-start | bytes 491528 | tf_op jit(solution)/shard_map/ppermute | solution.py:261
  94.4 2.0 %collective-permute-start.15 = (bf16[64,1280]{1,0:T(8,128)(2,1)S(1)}, bf16[64,1280]{1,0:T(8,128)(2,1)S(1)}, u32[]{:S(2)}, u32[]{:S(2)}) collective-permute-start(bf16[64,1280]{1,0:T(8,128)(2,1)S(1)} %collective-permute-done.11.refs_3_), channel_id=1, source_target_pairs={{0,4},{1,13},{2,6},{3,15},{4,8},{5,1},{6,10},{7,3},{8,12},{9,5},{1... | collective-permute-start | bytes 491528 | tf_op jit(solution)/shard_map/ppermute | solution.py:261
  96.4 2.4 %collective-permute-start.13 = (bf16[64,1280]{1,0:T(8,128)(2,1)S(1)}, bf16[64,1280]{1,0:T(8,128)(2,1)S(1)}, u32[]{:S(2)}, u32[]{:S(2)}) collective-permute-start(bf16[64,1280]{1,0:T(8,128)(2,1)S(1)} %collective-permute-done.9.refs_1_), channel_id=1, source_target_pairs={{0,4},{1,13},{2,6},{3,15},{4,8},{5,1},{6,10},{7,3},{8,12},{9,5},{1... | collective-permute-start | bytes 491528 | tf_op jit(solution)/shard_map/ppermute | solution.py:261
  99.2 3.3 %collective-permute-done.15.refs_7_ = bf16[64,1280]{1,0:T(8,128)(2,1)S(1)} collective-permute-done((bf16[64,1280]{1,0:T(8,128)(2,1)S(1)}, bf16[64,1280]{1,0:T(8,128)(2,1)S(1)}, u32[]{:S(2)}, u32[]{:S(2)}) %collective-permute-start.15) | collective-permute-done | bytes 163872 | tf_op jit(solution)/shard_map/ppermute | solution.py:261
  102.6 4.4 %collective-permute-done.13.refs_5_ = bf16[64,1280]{1,0:T(8,128)(2,1)S(1)} collective-permute-done((bf16[64,1280]{1,0:T(8,128)(2,1)S(1)}, bf16[64,1280]{1,0:T(8,128)(2,1)S(1)}, u32[]{:S(2)}, u32[]{:S(2)}) %collective-permute-start.13) | collective-permute-done | bytes 163872 | tf_op jit(solution)/shard_map/ppermute | solution.py:261
  107.0 2.8 %shard_map.116 = f32[16,128]{1,0:T(8,128)S(1)} custom-call(s32[1,2,4]{2,1,0:T(2,128)S(1)} %bitcast.11, s32[1,4]{1,0:T(1,128)S(1)} %copy-done.5, bf16[5120,256]{1,0:T(8,128)(2,1)S(1)} %copy-done, bf16[5120,256]{1,0:T(8,128)(2,1)} %collective-permute-done.8.wb_ref, bf16[64,1280]{1,0:T(8,128)(2,1)S(1)} %get-tuple-element.9.refs_0_, ...), custom_call_target="tpu_custom_call" | custom-call | flops 536870912 | bytes 7340032 | tf_op jit(solution)/shard_map/pallas_call | solution.py:353
  109.8 13.7 %all_to_all.21 = f32[16,1,128]{2,1,0:T(1,128)S(1)} all-to-all(f32[16,1,128]{2,1,0:T(1,128)S(1)} %bitcast.7), channel_id=1, replica_groups=mesh['rows'=32,'seq'=16] {'seq'}, dimensions={0} | all-to-all | bytes 16384 | tf_op jit(solution)/shard_map/all_to_all | solution.py:361
  (33 shorter events, 13.5 us)
Async XLA Ops:
  0.6 45.8 %copy-start.2 = (s32[1,4,2]{1,2,0:T(2,128)S(1)}, s32[1,4,2]{1,2,0:T(2,128)}, u32[]{:S(2)}) copy-start(s32[1,4,2]{1,2,0:T(2,128)} %param.13) | copy-start | bytes 100
  0.6 106.3 %collective-permute-start.8 = (bf16[5120,256]{1,0:T(8,128)(2,1)}, bf16[5120,256]{1,0:T(8,128)(2,1)}, u32[]{:S(2)}, u32[]{:S(2)}) collective-permute-start(bf16[5120,256]{1,0:T(8,128)(2,1)} %wa_ref.1), channel_id=1, source_target_pairs={{0,1},{1,0},{2,3},{3,2},{4,5},{5,4},{6,7},{7,6},{8,9},{9,8},{10,11... | collective-permute-start | bytes 7864328 | tf_op jit(solution)/shard_map/ppermute | solution.py:252
  9.4 55.3 %copy-start.1 = (bf16[1,64,1280]{2,1,0:T(8,128)(2,1)S(1)}, bf16[1,64,1280]{2,1,0:T(8,128)(2,1)}, u32[]{:S(2)}) copy-start(bf16[1,64,1280]{2,1,0:T(8,128)(2,1)} %hidden_ref.1) | copy-start | bytes 491524
  13.2 33.2 %all-to-all-start = ((bf16[16,64,256]{2,1,0:T(8,128)(2,1)}), bf16[16,64,256]{2,1,0:T(8,128)(2,1)S(1)}, u32[]{:S(2)}, u32[]{:S(2)}) async-start(bf16[16,64,256]{2,1,0:T(8,128)(2,1)} %shard_map.112), calls=%async_computation | async-start | bytes 1048576 | tf_op jit(solution)/shard_map/all_to_all | solution.py:307
  16.7 13.9 %collective-permute-start.3 = (bf16[40,1280]{1,0:T(8,128)(2,1)}, bf16[40,1280]{1,0:T(8,128)(2,1)S(1)}, u32[]{:S(2)}, u32[]{:S(2)}) collective-permute-start(bf16[40,1280]{1,0:T(8,128)(2,1)} %param.15), channel_id=1, source_target_pairs={{0,256},{2,258},{4,260},{6,262},{8,264},{10,266},{12,268},{14,270}... | collective-permute-start | bytes 307208 | tf_op jit(solution)/shard_map/ppermute | solution.py:261
  17.4 14.7 %collective-permute-start.2 = (bf16[40,1280]{1,0:T(8,128)(2,1)}, bf16[40,1280]{1,0:T(8,128)(2,1)S(1)}, u32[]{:S(2)}, u32[]{:S(2)}) collective-permute-start(bf16[40,1280]{1,0:T(8,128)(2,1)} %param.15), channel_id=1, source_target_pairs={{0,192},{1,321},{2,194},{3,323},{4,196},{5,325},{6,198},{7,327},{8... | collective-permute-start | bytes 307208 | tf_op jit(solution)/shard_map/ppermute | solution.py:261
  26.4 8.7 %collective-permute-start.1 = (bf16[40,1280]{1,0:T(8,128)(2,1)}, bf16[40,1280]{1,0:T(8,128)(2,1)S(1)}, u32[]{:S(2)}, u32[]{:S(2)}) collective-permute-start(bf16[40,1280]{1,0:T(8,128)(2,1)} %param.15), channel_id=1, source_target_pairs={{0,128},{1,385},{2,130},{3,387},{4,132},{5,389},{6,134},{7,391},{8... | collective-permute-start | bytes 307208 | tf_op jit(solution)/shard_map/ppermute | solution.py:261
  28.4 8.0 %collective-permute-start = (bf16[40,1280]{1,0:T(8,128)(2,1)}, bf16[40,1280]{1,0:T(8,128)(2,1)S(1)}, u32[]{:S(2)}, u32[]{:S(2)}) collective-permute-start(bf16[40,1280]{1,0:T(8,128)(2,1)} %param.15), channel_id=1, source_target_pairs={{0,64},{1,449},{2,66},{3,451},{4,68},{5,453},{6,70},{7,455},{8,72}... | collective-permute-start | bytes 307208 | tf_op jit(solution)/shard_map/ppermute | solution.py:261
  36.4 41.2 %copy-start.3 = (f32[1280]{0:T(1024)S(1)}, f32[1280]{0:T(1024)}, u32[]{:S(2)}) copy-start(f32[1280]{0:T(1024)} %gain_ref.1) | copy-start | bytes 15364
  36.4 41.2 %copy-start.4 = (f32[1280]{0:T(1024)S(1)}, f32[1280]{0:T(1024)}, u32[]{:S(2)}) copy-start(f32[1280]{0:T(1024)} %bias_ref.1) | copy-start | bytes 15364
  36.4 20.0 %collective-permute-start.6 = (bf16[160,1280]{1,0:T(8,128)(2,1)S(1)}, bf16[160,1280]{1,0:T(8,128)(2,1)}, u32[]{:S(2)}, u32[]{:S(2)}) collective-permute-start(bf16[160,1280]{1,0:T(8,128)(2,1)S(1)} %pad_maximum_fusion.own_ref), channel_id=1, source_target_pairs={{0,32},{16,48},{32,0},{48,16},{64,96},{80,112},{96,64},{112,80},{1... | collective-permute-start | bytes 1228808 | tf_op jit(solution)/shard_map/ppermute | solution.py:279
  41.1 15.4 %collective-permute-start.5 = (bf16[160,1280]{1,0:T(8,128)(2,1)S(1)}, bf16[160,1280]{1,0:T(8,128)(2,1)}, u32[]{:S(2)}, u32[]{:S(2)}) collective-permute-start(bf16[160,1280]{1,0:T(8,128)(2,1)S(1)} %pad_maximum_fusion.own_ref), channel_id=1, source_target_pairs={{0,48},{16,0},{32,16},{48,32},{64,112},{80,64},{96,80},{112,96},{1... | collective-permute-start | bytes 1228808 | tf_op jit(solution)/shard_map/ppermute | solution.py:279
  43.9 15.1 %collective-permute-start.4 = (bf16[160,1280]{1,0:T(8,128)(2,1)S(1)}, bf16[160,1280]{1,0:T(8,128)(2,1)}, u32[]{:S(2)}, u32[]{:S(2)}) collective-permute-start(bf16[160,1280]{1,0:T(8,128)(2,1)S(1)} %pad_maximum_fusion.own_ref), channel_id=1, source_target_pairs={{0,16},{16,32},{32,48},{48,0},{64,80},{80,96},{96,112},{112,64},{1... | collective-permute-start | bytes 1228808 | tf_op jit(solution)/shard_map/ppermute | solution.py:279
  49.5 57.5 %copy-start = (bf16[5120,256]{1,0:T(8,128)(2,1)S(1)}, bf16[5120,256]{1,0:T(8,128)(2,1)}, u32[]{:S(2)}) copy-start(bf16[5120,256]{1,0:T(8,128)(2,1)} %wa_ref.1) | copy-start | bytes 7864324
  49.5 57.5 %copy-start.5 = (s32[1,4]{1,0:T(1,128)S(1)}, s32[1,4]{1,0:T(1,128)}, u32[]{:S(2)}) copy-start(s32[1,4]{1,0:T(1,128)} %owner_ref.3) | copy-start | bytes 52
  49.5 15.2 %all-to-all-start.1 = ((bf16[8,2,40,128]{3,2,1,0:T(8,128)(2,1)}), bf16[8,2,40,128]{3,2,1,0:T(8,128)(2,1)S(1)}, u32[]{:S(2)}, u32[]{:S(2)}) async-start(bf16[8,2,40,128]{3,2,1,0:T(8,128)(2,1)} %shard_map.113), calls=%async_computation.1 | async-start | bytes 327680 | tf_op jit(solution)/shard_map/all_to_all | solution.py:317
  66.4 11.1 %collective-permute-start.7 = (f32[128,1280]{1,0:T(8,128)S(1)}, f32[128,1280]{1,0:T(8,128)S(1)}, u32[]{:S(2)}, u32[]{:S(2)}) collective-permute-start(f32[128,1280]{1,0:T(8,128)S(1)} %shard_map.114.own_ref), channel_id=1, source_target_pairs={{0,1},{1,0},{2,3},{3,2},{4,5},{5,4},{6,7},{7,6},{8,9},{9,8},{10,11... | collective-permute-start | bytes 1966088 | tf_op jit(solution)/shard_map/ppermute | solution.py:252
  78.6 11.6 %collective-permute-start.10 = (bf16[64,1280]{1,0:T(8,128)(2,1)S(1)}, bf16[64,1280]{1,0:T(8,128)(2,1)S(1)}, u32[]{:S(2)}, u32[]{:S(2)}) collective-permute-start(bf16[64,1280]{1,0:T(8,128)(2,1)S(1)} %get-tuple-element.10), channel_id=1, source_target_pairs={{0,2},{1,15},{2,4},{3,1},{4,6},{5,3},{6,8},{7,5},{8,10},{9,7},{10,... | collective-permute-start | bytes 491528 | tf_op jit(solution)/shard_map/ppermute | solution.py:261
  80.6 13.9 %collective-permute-start.11 = (bf16[64,1280]{1,0:T(8,128)(2,1)S(1)}, bf16[64,1280]{1,0:T(8,128)(2,1)S(1)}, u32[]{:S(2)}, u32[]{:S(2)}) collective-permute-start(bf16[64,1280]{1,0:T(8,128)(2,1)S(1)} %get-tuple-element.9.refs_0_), channel_id=1, source_target_pairs={{0,4},{1,13},{2,6},{3,15},{4,8},{5,1},{6,10},{7,3},{8,12},{9,5},{1... | collective-permute-start | bytes 491528 | tf_op jit(solution)/shard_map/ppermute | solution.py:261
  82.6 13.8 %collective-permute-start.9 = (bf16[64,1280]{1,0:T(8,128)(2,1)S(1)}, bf16[64,1280]{1,0:T(8,128)(2,1)S(1)}, u32[]{:S(2)}, u32[]{:S(2)}) collective-permute-start(bf16[64,1280]{1,0:T(8,128)(2,1)S(1)} %get-tuple-element.9.refs_0_), channel_id=1, source_target_pairs={{0,2},{1,15},{2,4},{3,1},{4,6},{5,3},{6,8},{7,5},{8,10},{9,7},{10,... | collective-permute-start | bytes 491528 | tf_op jit(solution)/shard_map/ppermute | solution.py:261
  85.2 13.6 %collective-permute-start.12 = (bf16[64,1280]{1,0:T(8,128)(2,1)S(1)}, bf16[64,1280]{1,0:T(8,128)(2,1)S(1)}, u32[]{:S(2)}, u32[]{:S(2)}) collective-permute-start(bf16[64,1280]{1,0:T(8,128)(2,1)S(1)} %get-tuple-element.10), channel_id=1, source_target_pairs={{0,4},{1,13},{2,6},{3,15},{4,8},{5,1},{6,10},{7,3},{8,12},{9,5},{1... | collective-permute-start | bytes 491528 | tf_op jit(solution)/shard_map/ppermute | solution.py:261
  90.2 9.0 %collective-permute-start.14 = (bf16[64,1280]{1,0:T(8,128)(2,1)S(1)}, bf16[64,1280]{1,0:T(8,128)(2,1)S(1)}, u32[]{:S(2)}, u32[]{:S(2)}) collective-permute-start(bf16[64,1280]{1,0:T(8,128)(2,1)S(1)} %collective-permute-done.10.refs_2_), channel_id=1, source_target_pairs={{0,4},{1,13},{2,6},{3,15},{4,8},{5,1},{6,10},{7,3},{8,12},{9,5},{1... | collective-permute-start | bytes 491528 | tf_op jit(solution)/shard_map/ppermute | solution.py:261
  94.4 8.1 %collective-permute-start.15 = (bf16[64,1280]{1,0:T(8,128)(2,1)S(1)}, bf16[64,1280]{1,0:T(8,128)(2,1)S(1)}, u32[]{:S(2)}, u32[]{:S(2)}) collective-permute-start(bf16[64,1280]{1,0:T(8,128)(2,1)S(1)} %collective-permute-done.11.refs_3_), channel_id=1, source_target_pairs={{0,4},{1,13},{2,6},{3,15},{4,8},{5,1},{6,10},{7,3},{8,12},{9,5},{1... | collective-permute-start | bytes 491528 | tf_op jit(solution)/shard_map/ppermute | solution.py:261
  96.4 10.5 %collective-permute-start.13 = (bf16[64,1280]{1,0:T(8,128)(2,1)S(1)}, bf16[64,1280]{1,0:T(8,128)(2,1)S(1)}, u32[]{:S(2)}, u32[]{:S(2)}) collective-permute-start(bf16[64,1280]{1,0:T(8,128)(2,1)S(1)} %collective-permute-done.9.refs_1_), channel_id=1, source_target_pairs={{0,4},{1,13},{2,6},{3,15},{4,8},{5,1},{6,10},{7,3},{8,12},{9,5},{1... | collective-permute-start | bytes 491528 | tf_op jit(solution)/shard_map/ppermute | solution.py:261

commit v2 on v1

--- a/solution.py
+++ b/solution.py
@@ -266,13 +266,14 @@
         row, place = index // 16, index % 16
         return (row + 4 * step) % 32 * 16 + place
 
-    blocks = []
-    for k in range(1, 5):
-        cores = (0, 1) if k < 4 else (0,)
-        blocks.append(two_way(("rows", "seq"), weight, move, 512, k, cores))
+    def send(value, places, cores=(0, 1)):
+        return two_way(("rows", "seq"), value, move, 512, places, cores)
+
+    one = send(weight, 1)
+    four = send(weight, 4, (0,))
+    two = send(jnp.concatenate([weight, one], axis=0), 2)
     core = lax.axis_index("seq") & 1
-    blocks[3] = jnp.where(core == 0, blocks[3], weight)
-    bundle = jnp.concatenate(blocks, axis=0)
+    bundle = jnp.concatenate([one, two, jnp.where(core == 0, four, weight)], axis=0)
 
     def shift_x(step):
         pairs = [(r, (r & ~3) + ((r + step) & 3)) for r in range(32)]

time: 125 us -> 126 us (level)
  starting transfers between devices: 72.5 us -> 70.3 us
  waiting for transfers between devices: 22.9 us -> 24.7 us
    all_to_all x1, starting transfers between devices: 3.47 us -> 10.2 us  [body(): lax.all_to_all(packed, 'seq', split_axis=0, concat_axis=0, tiled=True)]
    ppermute x11 -> x10, starting transfers between devices: 34 us -> 28.1 us  [two_way(): return lax.ppermute(value, axes, pairs)]
    ppermute x2, starting transfers between devices: 18.2 us -> 15.3 us  [chip_shift(): return lax.ppermute(x, 'seq', pairs)]
    ppermute x11 -> x10, waiting for transfers between devices: 13 us -> 14.6 us  [two_way(): return lax.ppermute(value, axes, pairs)]
  transfers between devices with their start and end apart: 18 -> 17, of which waited for: 10 -> 7; matrix products, arithmetic and copies ran while one was open for 1% -> 1% of each run, Pallas kernels for 8% -> 8%
where the time goes in v2:
time: 126 us
  starting transfers between devices  70.3 us (56%)
  waiting for transfers between devices  24.7 us (20%)
  blocking collectives  14.2 us (11%)
  Pallas kernels  13.6 us (11%)
  other arithmetic  1.86 us (1%)
    ppermute x10, starting transfers between devices, two_way(): return lax.ppermute(value, axes, pairs)  28.1 us
    ppermute x2, starting transfers between devices, chip_shift(): return lax.ppermute(x, 'seq', pairs)  15.3 us
    ppermute x10, waiting for transfers between devices, two_way(): return lax.ppermute(value, axes, pairs)  14.6 us
    all_to_all x1, blocking collectives, body(): lax.all_to_all(stats, 'seq', split_axis=0, concat_axis=0, tiled=True)  14.2 us
    all_to_all x1, starting transfers between devices, body(): lax.all_to_all(packed, 'seq', split_axis=0, concat_axis=0, tiled=True)  10.2 us
    ppermute x3, starting transfers between devices, shift_x(): return lax.ppermute(bundle, 'rows', pairs)  9.94 us
    all_to_all x1, starting transfers between devices, body(): lax.all_to_all(head_out, 'seq', split_axis=0, concat_axis=0, axis_index_g...  6.8 us
    all_to_all x1, waiting for transfers between devices, body(): lax.all_to_all(head_out, 'seq', split_axis=0, concat_axis=0, axis_index_g...  5.55 us
  transfers between devices with their start and end apart: 17, of which 7 were waited for; matrix products, arithmetic and copies ran while one was open for 1% of the time, Pallas kernels for 8%

profile of v2, /device:TPU:1, one launch (start us, length us, event | category | flops | bytes accessed | tf_op | source)
XLA Modules:
  0.0 125.5 jit_solution(2986756587779495876)
XLA Ops:
  0.6 8.8 %collective-permute-start.7 = (bf16[5120,256]{1,0:T(8,128)(2,1)}, bf16[5120,256]{1,0:T(8,128)(2,1)}, u32[]{:S(2)}, u32[]{:S(2)}) collective-permute-start(bf16[5120,256]{1,0:T(8,128)(2,1)} %wa_ref.1), channel_id=1, source_target_pairs={{0,1},{1,0},{2,3},{3,2},{4,5},{5,4},{6,7},{7,6},{8,9},{9,8},{10,11... | collective-permute-start | bytes 7864328 | tf_op jit(solution)/shard_map/ppermute | solution.py:252
  9.4 5.3 %collective-permute-start = (bf16[40,1280]{1,0:T(8,128)(2,1)}, bf16[40,1280]{1,0:T(8,128)(2,1)S(1)}, u32[]{:S(2)}, u32[]{:S(2)}) collective-permute-start(bf16[40,1280]{1,0:T(8,128)(2,1)} %param.15), channel_id=1, source_target_pairs={{0,64},{1,449},{2,66},{3,451},{4,68},{5,453},{6,70},{7,455},{8,72}... | collective-permute-start | bytes 307208 | tf_op jit(solution)/shard_map/ppermute | solution.py:261
  15.4 3.8 %shard_map.112 = bf16[16,64,256]{2,1,0:T(8,128)(2,1)} custom-call(s32[1,2,4]{2,1,0:T(2,128)} %bitcast.9, s32[1,64]{1,0:T(1,128)} %keep_ref.1, bf16[1,64,3840]{2,1,0:T(8,128)(2,1)} %qkv_ref.1), custom_call_target="tpu_custom_call" | custom-call | flops 4194304 | bytes 1048576 | tf_op jit(solution)/shard_map/pallas_call | solution.py:300
  19.2 10.2 %all-to-all-start = ((bf16[16,64,256]{2,1,0:T(8,128)(2,1)}), bf16[16,64,256]{2,1,0:T(8,128)(2,1)S(1)}, u32[]{:S(2)}, u32[]{:S(2)}) async-start(bf16[16,64,256]{2,1,0:T(8,128)(2,1)} %shard_map.112), calls=%async_computation | async-start | bytes 1048576 | tf_op jit(solution)/shard_map/all_to_all | solution.py:308
  30.3 1.9 %collective-permute-start.1 = (bf16[80,1280]{1,0:T(8,128)(2,1)S(1)}, bf16[80,1280]{1,0:T(8,128)(2,1)S(1)}, u32[]{:S(2)}, u32[]{:S(2)}) collective-permute-start(bf16[80,1280]{1,0:T(8,128)(2,1)S(1)} %pad_maximum_fusion.1), channel_id=1, source_target_pairs={{0,128},{1,385},{2,130},{3,387},{4,132},{5,389},{6,134},{7,391},{8... | collective-permute-start | bytes 614408 | tf_op jit(solution)/shard_map/ppermute | solution.py:261
  33.2 7.0 %collective-permute-done.1 = bf16[80,1280]{1,0:T(8,128)(2,1)S(1)} collective-permute-done((bf16[80,1280]{1,0:T(8,128)(2,1)S(1)}, bf16[80,1280]{1,0:T(8,128)(2,1)S(1)}, u32[]{:S(2)}, u32[]{:S(2)}) %collective-permute-start.1) | collective-permute-done | bytes 204832 | tf_op jit(solution)/shard_map/ppermute | solution.py:261
  40.3 4.7 %collective-permute-start.5 = (bf16[160,1280]{1,0:T(8,128)(2,1)S(1)}, bf16[160,1280]{1,0:T(8,128)(2,1)}, u32[]{:S(2)}, u32[]{:S(2)}) collective-permute-start(bf16[160,1280]{1,0:T(8,128)(2,1)S(1)} %pad_maximum_fusion.own_ref), channel_id=1, source_target_pairs={{0,32},{16,48},{32,0},{48,16},{64,96},{80,112},{96,64},{112,80},{1... | collective-permute-start | bytes 1228808 | tf_op jit(solution)/shard_map/ppermute | solution.py:280
  44.9 2.8 %collective-permute-start.4 = (bf16[160,1280]{1,0:T(8,128)(2,1)S(1)}, bf16[160,1280]{1,0:T(8,128)(2,1)}, u32[]{:S(2)}, u32[]{:S(2)}) collective-permute-start(bf16[160,1280]{1,0:T(8,128)(2,1)S(1)} %pad_maximum_fusion.own_ref), channel_id=1, source_target_pairs={{0,48},{16,0},{32,16},{48,32},{64,112},{80,64},{96,80},{112,96},{1... | collective-permute-start | bytes 1228808 | tf_op jit(solution)/shard_map/ppermute | solution.py:280
  47.7 2.5 %collective-permute-start.3 = (bf16[160,1280]{1,0:T(8,128)(2,1)S(1)}, bf16[160,1280]{1,0:T(8,128)(2,1)}, u32[]{:S(2)}, u32[]{:S(2)}) collective-permute-start(bf16[160,1280]{1,0:T(8,128)(2,1)S(1)} %pad_maximum_fusion.own_ref), channel_id=1, source_target_pairs={{0,16},{16,32},{32,48},{48,0},{64,80},{80,96},{96,112},{112,64},{1... | collective-permute-start | bytes 1228808 | tf_op jit(solution)/shard_map/ppermute | solution.py:280
  50.3 3.1 %shard_map.113 = bf16[8,2,40,128]{3,2,1,0:T(8,128)(2,1)} custom-call(s32[1,2,4]{2,1,0:T(2,128)S(1)} %bitcast.10, bf16[1024,256]{1,0:T(8,128)(2,1)S(1)} %bitcast.6), custom_call_target="tpu_custom_call" | custom-call | flops 536870912 | bytes 1048576 | tf_op jit(solution)/shard_map/pallas_call | solution.py:310
  53.3 6.8 %all-to-all-start.1 = ((bf16[8,2,40,128]{3,2,1,0:T(8,128)(2,1)}), bf16[8,2,40,128]{3,2,1,0:T(8,128)(2,1)S(1)}, u32[]{:S(2)}, u32[]{:S(2)}) async-start(bf16[8,2,40,128]{3,2,1,0:T(8,128)(2,1)} %shard_map.113), calls=%async_computation.1 | async-start | bytes 327680 | tf_op jit(solution)/shard_map/all_to_all | solution.py:318
  60.1 2.8 %collective-permute-done.4.minus_ref = bf16[160,1280]{1,0:T(8,128)(2,1)} collective-permute-done((bf16[160,1280]{1,0:T(8,128)(2,1)S(1)}, bf16[160,1280]{1,0:T(8,128)(2,1)}, u32[]{:S(2)}, u32[]{:S(2)}) %collective-permute-start.4) | collective-permute-done | bytes 409632 | tf_op jit(solution)/shard_map/ppermute | solution.py:280
  62.9 5.6 %all-to-all-done.1.heads_ref = bf16[8,2,40,128]{3,2,1,0:T(8,128)(2,1)S(1)} async-done(((bf16[8,2,40,128]{3,2,1,0:T(8,128)(2,1)}), bf16[8,2,40,128]{3,2,1,0:T(8,128)(2,1)S(1)}, u32[]{:S(2)}, u32[]{:S(2)}) %all-to-all-start.1) | async-done | bytes 163872 | tf_op jit(solution)/shard_map/all_to_all | solution.py:318
  70.3 6.5 %collective-permute-start.6 = (f32[128,1280]{1,0:T(8,128)S(1)}, f32[128,1280]{1,0:T(8,128)S(1)}, u32[]{:S(2)}, u32[]{:S(2)}) collective-permute-start(f32[128,1280]{1,0:T(8,128)S(1)} %shard_map.114.own_ref), channel_id=1, source_target_pairs={{0,1},{1,0},{2,3},{3,2},{4,5},{5,4},{6,7},{7,6},{8,9},{9,8},{10,11... | collective-permute-start | bytes 1966088 | tf_op jit(solution)/shard_map/ppermute | solution.py:252
  81.5 2.0 %collective-permute-start.10 = (bf16[64,1280]{1,0:T(8,128)(2,1)S(1)}, bf16[64,1280]{1,0:T(8,128)(2,1)S(1)}, u32[]{:S(2)}, u32[]{:S(2)}) collective-permute-start(bf16[64,1280]{1,0:T(8,128)(2,1)S(1)} %get-tuple-element.9.refs_0_), channel_id=1, source_target_pairs={{0,4},{1,13},{2,6},{3,15},{4,8},{5,1},{6,10},{7,3},{8,12},{9,5},{1... | collective-permute-start | bytes 491528 | tf_op jit(solution)/shard_map/ppermute | solution.py:261
  83.5 2.6 %collective-permute-start.8 = (bf16[64,1280]{1,0:T(8,128)(2,1)S(1)}, bf16[64,1280]{1,0:T(8,128)(2,1)S(1)}, u32[]{:S(2)}, u32[]{:S(2)}) collective-permute-start(bf16[64,1280]{1,0:T(8,128)(2,1)S(1)} %get-tuple-element.9.refs_0_), channel_id=1, source_target_pairs={{0,2},{1,15},{2,4},{3,1},{4,6},{5,3},{6,8},{7,5},{8,10},{9,7},{10,... | collective-permute-start | bytes 491528 | tf_op jit(solution)/shard_map/ppermute | solution.py:261
  86.2 4.4 %collective-permute-start.11 = (bf16[64,1280]{1,0:T(8,128)(2,1)S(1)}, bf16[64,1280]{1,0:T(8,128)(2,1)S(1)}, u32[]{:S(2)}, u32[]{:S(2)}) collective-permute-start(bf16[64,1280]{1,0:T(8,128)(2,1)S(1)} %get-tuple-element.10), channel_id=1, source_target_pairs={{0,4},{1,13},{2,6},{3,15},{4,8},{5,1},{6,10},{7,3},{8,12},{9,5},{1... | collective-permute-start | bytes 491528 | tf_op jit(solution)/shard_map/ppermute | solution.py:261
  90.6 4.8 %collective-permute-start.13 = (bf16[64,1280]{1,0:T(8,128)(2,1)S(1)}, bf16[64,1280]{1,0:T(8,128)(2,1)S(1)}, u32[]{:S(2)}, u32[]{:S(2)}) collective-permute-start(bf16[64,1280]{1,0:T(8,128)(2,1)S(1)} %collective-permute-done.9.refs_2_), channel_id=1, source_target_pairs={{0,4},{1,13},{2,6},{3,15},{4,8},{5,1},{6,10},{7,3},{8,12},{9,5},{1... | collective-permute-start | bytes 491528 | tf_op jit(solution)/shard_map/ppermute | solution.py:261
  95.4 2.0 %collective-permute-start.14 = (bf16[64,1280]{1,0:T(8,128)(2,1)S(1)}, bf16[64,1280]{1,0:T(8,128)(2,1)S(1)}, u32[]{:S(2)}, u32[]{:S(2)}) collective-permute-start(bf16[64,1280]{1,0:T(8,128)(2,1)S(1)} %collective-permute-done.10.refs_3_), channel_id=1, source_target_pairs={{0,4},{1,13},{2,6},{3,15},{4,8},{5,1},{6,10},{7,3},{8,12},{9,5},{1... | collective-permute-start | bytes 491528 | tf_op jit(solution)/shard_map/ppermute | solution.py:261
  97.4 2.4 %collective-permute-start.12 = (bf16[64,1280]{1,0:T(8,128)(2,1)S(1)}, bf16[64,1280]{1,0:T(8,128)(2,1)S(1)}, u32[]{:S(2)}, u32[]{:S(2)}) collective-permute-start(bf16[64,1280]{1,0:T(8,128)(2,1)S(1)} %collective-permute-done.8.refs_1_), channel_id=1, source_target_pairs={{0,4},{1,13},{2,6},{3,15},{4,8},{5,1},{6,10},{7,3},{8,12},{9,5},{1... | collective-permute-start | bytes 491528 | tf_op jit(solution)/shard_map/ppermute | solution.py:261
  100.6 2.2 %collective-permute-done.14.refs_7_ = bf16[64,1280]{1,0:T(8,128)(2,1)S(1)} collective-permute-done((bf16[64,1280]{1,0:T(8,128)(2,1)S(1)}, bf16[64,1280]{1,0:T(8,128)(2,1)S(1)}, u32[]{:S(2)}, u32[]{:S(2)}) %collective-permute-start.14) | collective-permute-done | bytes 163872 | tf_op jit(solution)/shard_map/ppermute | solution.py:261
  102.8 4.5 %collective-permute-done.12.refs_5_ = bf16[64,1280]{1,0:T(8,128)(2,1)S(1)} collective-permute-done((bf16[64,1280]{1,0:T(8,128)(2,1)S(1)}, bf16[64,1280]{1,0:T(8,128)(2,1)S(1)}, u32[]{:S(2)}, u32[]{:S(2)}) %collective-permute-start.12) | collective-permute-done | bytes 163872 | tf_op jit(solution)/shard_map/ppermute | solution.py:261
  107.4 2.8 %shard_map.116 = f32[16,128]{1,0:T(8,128)S(1)} custom-call(s32[1,2,4]{2,1,0:T(2,128)S(1)} %bitcast.11, s32[1,4]{1,0:T(1,128)S(1)} %copy-done.5, bf16[5120,256]{1,0:T(8,128)(2,1)S(1)} %copy-done, bf16[5120,256]{1,0:T(8,128)(2,1)} %collective-permute-done.7.wb_ref, bf16[64,1280]{1,0:T(8,128)(2,1)S(1)} %get-tuple-element.9.refs_0_, ...), custom_call_target="tpu_custom_call" | custom-call | flops 536870912 | bytes 7340032 | tf_op jit(solution)/shard_map/pallas_call | solution.py:354
  110.1 14.2 %all_to_all.21 = f32[16,1,128]{2,1,0:T(1,128)S(1)} all-to-all(f32[16,1,128]{2,1,0:T(1,128)S(1)} %bitcast.7), channel_id=1, replica_groups=mesh['rows'=32,'seq'=16] {'seq'}, dimensions={0} | all-to-all | bytes 16384 | tf_op jit(solution)/shard_map/all_to_all | solution.py:362
  (32 shorter events, 11.0 us)
Async XLA Ops:
  0.6 49.6 %copy-start.2 = (s32[1,4,2]{1,2,0:T(2,128)S(1)}, s32[1,4,2]{1,2,0:T(2,128)}, u32[]{:S(2)}) copy-start(s32[1,4,2]{1,2,0:T(2,128)} %param.13) | copy-start | bytes 100
  0.6 106.7 %collective-permute-start.7 = (bf16[5120,256]{1,0:T(8,128)(2,1)}, bf16[5120,256]{1,0:T(8,128)(2,1)}, u32[]{:S(2)}, u32[]{:S(2)}) collective-permute-start(bf16[5120,256]{1,0:T(8,128)(2,1)} %wa_ref.1), channel_id=1, source_target_pairs={{0,1},{1,0},{2,3},{3,2},{4,5},{5,4},{6,7},{7,6},{8,9},{9,8},{10,11... | collective-permute-start | bytes 7864328 | tf_op jit(solution)/shard_map/ppermute | solution.py:252
  9.4 20.0 %collective-permute-start = (bf16[40,1280]{1,0:T(8,128)(2,1)}, bf16[40,1280]{1,0:T(8,128)(2,1)S(1)}, u32[]{:S(2)}, u32[]{:S(2)}) collective-permute-start(bf16[40,1280]{1,0:T(8,128)(2,1)} %param.15), channel_id=1, source_target_pairs={{0,64},{1,449},{2,66},{3,451},{4,68},{5,453},{6,70},{7,455},{8,72}... | collective-permute-start | bytes 307208 | tf_op jit(solution)/shard_map/ppermute | solution.py:261
  14.7 17.5 %collective-permute-start.2 = (bf16[40,1280]{1,0:T(8,128)(2,1)}, bf16[40,1280]{1,0:T(8,128)(2,1)S(1)}, u32[]{:S(2)}, u32[]{:S(2)}) collective-permute-start(bf16[40,1280]{1,0:T(8,128)(2,1)} %param.15), channel_id=1, source_target_pairs={{0,256},{2,258},{4,260},{6,262},{8,264},{10,266},{12,268},{14,270}... | collective-permute-start | bytes 307208 | tf_op jit(solution)/shard_map/ppermute | solution.py:261
  19.2 49.3 %copy-start.1 = (bf16[1,64,1280]{2,1,0:T(8,128)(2,1)S(1)}, bf16[1,64,1280]{2,1,0:T(8,128)(2,1)}, u32[]{:S(2)}) copy-start(bf16[1,64,1280]{2,1,0:T(8,128)(2,1)} %hidden_ref.1) | copy-start | bytes 491524
  19.2 31.1 %all-to-all-start = ((bf16[16,64,256]{2,1,0:T(8,128)(2,1)}), bf16[16,64,256]{2,1,0:T(8,128)(2,1)S(1)}, u32[]{:S(2)}, u32[]{:S(2)}) async-start(bf16[16,64,256]{2,1,0:T(8,128)(2,1)} %shard_map.112), calls=%async_computation | async-start | bytes 1048576 | tf_op jit(solution)/shard_map/all_to_all | solution.py:308
  30.3 9.9 %collective-permute-start.1 = (bf16[80,1280]{1,0:T(8,128)(2,1)S(1)}, bf16[80,1280]{1,0:T(8,128)(2,1)S(1)}, u32[]{:S(2)}, u32[]{:S(2)}) collective-permute-start(bf16[80,1280]{1,0:T(8,128)(2,1)S(1)} %pad_maximum_fusion.1), channel_id=1, source_target_pairs={{0,128},{1,385},{2,130},{3,387},{4,132},{5,389},{6,134},{7,391},{8... | collective-permute-start | bytes 614408 | tf_op jit(solution)/shard_map/ppermute | solution.py:261
  40.3 38.3 %copy-start.3 = (f32[1280]{0:T(1024)S(1)}, f32[1280]{0:T(1024)}, u32[]{:S(2)}) copy-start(f32[1280]{0:T(1024)} %gain_ref.1) | copy-start | bytes 15364
  40.3 38.3 %copy-start.4 = (f32[1280]{0:T(1024)S(1)}, f32[1280]{0:T(1024)}, u32[]{:S(2)}) copy-start(f32[1280]{0:T(1024)} %bias_ref.1) | copy-start | bytes 15364
  40.3 19.8 %collective-permute-start.5 = (bf16[160,1280]{1,0:T(8,128)(2,1)S(1)}, bf16[160,1280]{1,0:T(8,128)(2,1)}, u32[]{:S(2)}, u32[]{:S(2)}) collective-permute-start(bf16[160,1280]{1,0:T(8,128)(2,1)S(1)} %pad_maximum_fusion.own_ref), channel_id=1, source_target_pairs={{0,32},{16,48},{32,0},{48,16},{64,96},{80,112},{96,64},{112,80},{1... | collective-permute-start | bytes 1228808 | tf_op jit(solution)/shard_map/ppermute | solution.py:280
  44.9 18.0 %collective-permute-start.4 = (bf16[160,1280]{1,0:T(8,128)(2,1)S(1)}, bf16[160,1280]{1,0:T(8,128)(2,1)}, u32[]{:S(2)}, u32[]{:S(2)}) collective-permute-start(bf16[160,1280]{1,0:T(8,128)(2,1)S(1)} %pad_maximum_fusion.own_ref), channel_id=1, source_target_pairs={{0,48},{16,0},{32,16},{48,32},{64,112},{80,64},{96,80},{112,96},{1... | collective-permute-start | bytes 1228808 | tf_op jit(solution)/shard_map/ppermute | solution.py:280
  47.7 15.2 %collective-permute-start.3 = (bf16[160,1280]{1,0:T(8,128)(2,1)S(1)}, bf16[160,1280]{1,0:T(8,128)(2,1)}, u32[]{:S(2)}, u32[]{:S(2)}) collective-permute-start(bf16[160,1280]{1,0:T(8,128)(2,1)S(1)} %pad_maximum_fusion.own_ref), channel_id=1, source_target_pairs={{0,16},{16,32},{32,48},{48,0},{64,80},{80,96},{96,112},{112,64},{1... | collective-permute-start | bytes 1228808 | tf_op jit(solution)/shard_map/ppermute | solution.py:280
  53.3 54.0 %copy-start = (bf16[5120,256]{1,0:T(8,128)(2,1)S(1)}, bf16[5120,256]{1,0:T(8,128)(2,1)}, u32[]{:S(2)}) copy-start(bf16[5120,256]{1,0:T(8,128)(2,1)} %wa_ref.1) | copy-start | bytes 7864324
  53.3 54.0 %copy-start.5 = (s32[1,4]{1,0:T(1,128)S(1)}, s32[1,4]{1,0:T(1,128)}, u32[]{:S(2)}) copy-start(s32[1,4]{1,0:T(1,128)} %owner_ref.3) | copy-start | bytes 52
  53.3 15.2 %all-to-all-start.1 = ((bf16[8,2,40,128]{3,2,1,0:T(8,128)(2,1)}), bf16[8,2,40,128]{3,2,1,0:T(8,128)(2,1)S(1)}, u32[]{:S(2)}, u32[]{:S(2)}) async-start(bf16[8,2,40,128]{3,2,1,0:T(8,128)(2,1)} %shard_map.113), calls=%async_computation.1 | async-start | bytes 327680 | tf_op jit(solution)/shard_map/all_to_all | solution.py:318
  70.3 8.2 %collective-permute-start.6 = (f32[128,1280]{1,0:T(8,128)S(1)}, f32[128,1280]{1,0:T(8,128)S(1)}, u32[]{:S(2)}, u32[]{:S(2)}) collective-permute-start(f32[128,1280]{1,0:T(8,128)S(1)} %shard_map.114.own_ref), channel_id=1, source_target_pairs={{0,1},{1,0},{2,3},{3,2},{4,5},{5,4},{6,7},{7,6},{8,9},{9,8},{10,11... | collective-permute-start | bytes 1966088 | tf_op jit(solution)/shard_map/ppermute | solution.py:252
  79.6 11.0 %collective-permute-start.9 = (bf16[64,1280]{1,0:T(8,128)(2,1)S(1)}, bf16[64,1280]{1,0:T(8,128)(2,1)S(1)}, u32[]{:S(2)}, u32[]{:S(2)}) collective-permute-start(bf16[64,1280]{1,0:T(8,128)(2,1)S(1)} %get-tuple-element.10), channel_id=1, source_target_pairs={{0,2},{1,15},{2,4},{3,1},{4,6},{5,3},{6,8},{7,5},{8,10},{9,7},{10,... | collective-permute-start | bytes 491528 | tf_op jit(solution)/shard_map/ppermute | solution.py:261
  81.5 13.9 %collective-permute-start.10 = (bf16[64,1280]{1,0:T(8,128)(2,1)S(1)}, bf16[64,1280]{1,0:T(8,128)(2,1)S(1)}, u32[]{:S(2)}, u32[]{:S(2)}) collective-permute-start(bf16[64,1280]{1,0:T(8,128)(2,1)S(1)} %get-tuple-element.9.refs_0_), channel_id=1, source_target_pairs={{0,4},{1,13},{2,6},{3,15},{4,8},{5,1},{6,10},{7,3},{8,12},{9,5},{1... | collective-permute-start | bytes 491528 | tf_op jit(solution)/shard_map/ppermute | solution.py:261
  83.5 13.8 %collective-permute-start.8 = (bf16[64,1280]{1,0:T(8,128)(2,1)S(1)}, bf16[64,1280]{1,0:T(8,128)(2,1)S(1)}, u32[]{:S(2)}, u32[]{:S(2)}) collective-permute-start(bf16[64,1280]{1,0:T(8,128)(2,1)S(1)} %get-tuple-element.9.refs_0_), channel_id=1, source_target_pairs={{0,2},{1,15},{2,4},{3,1},{4,6},{5,3},{6,8},{7,5},{8,10},{9,7},{10,... | collective-permute-start | bytes 491528 | tf_op jit(solution)/shard_map/ppermute | solution.py:261
  86.2 13.6 %collective-permute-start.11 = (bf16[64,1280]{1,0:T(8,128)(2,1)S(1)}, bf16[64,1280]{1,0:T(8,128)(2,1)S(1)}, u32[]{:S(2)}, u32[]{:S(2)}) collective-permute-start(bf16[64,1280]{1,0:T(8,128)(2,1)S(1)} %get-tuple-element.10), channel_id=1, source_target_pairs={{0,4},{1,13},{2,6},{3,15},{4,8},{5,1},{6,10},{7,3},{8,12},{9,5},{1... | collective-permute-start | bytes 491528 | tf_op jit(solution)/shard_map/ppermute | solution.py:261
  90.6 10.0 %collective-permute-start.13 = (bf16[64,1280]{1,0:T(8,128)(2,1)S(1)}, bf16[64,1280]{1,0:T(8,128)(2,1)S(1)}, u32[]{:S(2)}, u32[]{:S(2)}) collective-permute-start(bf16[64,1280]{1,0:T(8,128)(2,1)S(1)} %collective-permute-done.9.refs_2_), channel_id=1, source_target_pairs={{0,4},{1,13},{2,6},{3,15},{4,8},{5,1},{6,10},{7,3},{8,12},{9,5},{1... | collective-permute-start | bytes 491528 | tf_op jit(solution)/shard_map/ppermute | solution.py:261
  95.4 7.4 %collective-permute-start.14 = (bf16[64,1280]{1,0:T(8,128)(2,1)S(1)}, bf16[64,1280]{1,0:T(8,128)(2,1)S(1)}, u32[]{:S(2)}, u32[]{:S(2)}) collective-permute-start(bf16[64,1280]{1,0:T(8,128)(2,1)S(1)} %collective-permute-done.10.refs_3_), channel_id=1, source_target_pairs={{0,4},{1,13},{2,6},{3,15},{4,8},{5,1},{6,10},{7,3},{8,12},{9,5},{1... | collective-permute-start | bytes 491528 | tf_op jit(solution)/shard_map/ppermute | solution.py:261
  97.4 10.0 %collective-permute-start.12 = (bf16[64,1280]{1,0:T(8,128)(2,1)S(1)}, bf16[64,1280]{1,0:T(8,128)(2,1)S(1)}, u32[]{:S(2)}, u32[]{:S(2)}) collective-permute-start(bf16[64,1280]{1,0:T(8,128)(2,1)S(1)} %collective-permute-done.8.refs_1_), channel_id=1, source_target_pairs={{0,4},{1,13},{2,6},{3,15},{4,8},{5,1},{6,10},{7,3},{8,12},{9,5},{1... | collective-permute-start | bytes 491528 | tf_op jit(solution)/shard_map/ppermute | solution.py:261

commit v3 on v2

--- a/solution.py
+++ b/solution.py
@@ -43,10 +43,12 @@
     place = lax.axis_index("seq") * TOK + iota((TOK, 256), 0)
     begin = jnp.zeros((TOK, 256), jnp.int32)
     width = jnp.full((TOK, 256), 2, jnp.int32)
+    end = jnp.zeros((TOK, 256), jnp.int32)
     for j in range(IMGS):
         inside = (place >= starts[j]) & (place < ends[j])
         begin = jnp.where(inside, starts[j], begin)
         width = jnp.where(inside, grid_ref[0, 1, j], width)
+        end = jnp.where(inside, ends[j], end)
     valid = place < ends[IMGS - 1]
     offset = place - begin
     square = lax.shift_right_logical(offset, 2)
@@ -70,7 +72,10 @@
     sine = jnp.where(rotated, jnp.where(low, -sine, sine), 0.0)
     diagonal = iota((TOK, TOK), 0) == iota((TOK, TOK), 1)
     flags = jnp.where(diagonal, keep_ref[...].astype(F32), 0.0)
-    tail = jnp.broadcast_to(jnp.sum(flags, axis=1, keepdims=True), (TOK, 16))
+    spare = iota((TOK, 16), 1)
+    tail = jnp.where(spare == 0, jnp.sum(flags, axis=1, keepdims=True), 0.0)
+    tail = jnp.where(spare == 1, 0.25 * begin[:, :16].astype(F32), tail)
+    tail = jnp.where(spare == 2, 0.25 * end[:, :16].astype(F32), tail)
     z = lax.shift_right_logical(lax.axis_index("rows"), 2)
     for head in range(HEADS):
         behind = (z - head // 2) & 7
@@ -86,13 +91,12 @@
         out_ref[dest] = (full * cosine + swapped * sine).astype(BF16)
 
 
-def attention_kernel(grid_ref, x_ref, out_ref):
-    starts, ends = image_bounds(grid_ref)
+def attention_kernel(x_ref, out_ref):
     pick = jnp.where(iota((8, 128), 1) == 112, 1.0, 0.0).astype(BF16)
     keep = lax.dot_general(
         pick, x_ref[:, 128:], (((1,), (1,)), ((), ())), preferred_element_type=F32
     )[0:1]
-    key_place = jnp.where(keep > 0.5, iota((1, SEQ), 1), -1)
+    key_place = jnp.where(keep > 0.5, iota((1, SEQ), 1).astype(F32), -1.0)
     query_lane = iota((128, 128), 1) < HD
 
     def emit(chip, rows):
@@ -114,12 +118,8 @@
             preferred_element_type=F32,
         ) * HD ** (-0.5)
         place = first + iota((128, 1), 0)
-        lo = place
-        hi = place
-        for j in range(IMGS):
-            inside = (place >= starts[j]) & (place < ends[j])
-            lo = jnp.where(inside, starts[j], lo)
-            hi = jnp.where(inside, ends[j], hi)
+        bounds = 4.0 * x_ref[first : first + 128, 128:256].astype(F32)
+        lo, hi = bounds[:, 113:114], bounds[:, 114:115]
         keys = key_place[:, low:high]
         same = (keys >= lo) & (keys < hi)
         own = iota((1, high - low), 1) + low == place
@@ -154,7 +154,7 @@
 
 
 def norm_kernel(
-    own_ref, recv_ref, gain_ref, bias_ref, normed_ref, first_ref, second_ref, keep_ref
+    own_ref, recv_ref, gain_ref, bias_ref, normed_ref, block_ref, keep_ref
 ):
     mixed = own_ref[...] + recv_ref[...]
     centred = mixed - jnp.mean(mixed, axis=1, keepdims=True)
@@ -168,19 +168,19 @@
     half = (lax.shift_right_logical(line, 6) + core) & 1
     source = TOK * half + 4 * (line & 15) + (lax.shift_right_logical(line, 4) & 3)
     order = jnp.where(iota((128, 128), 1) == source, 1.0, 0.0).astype(BF16)
-    chunks = jnp.dot(order, normed, preferred_element_type=F32).astype(BF16)
-    first_ref[...] = chunks[:TOK]
-    second_ref[...] = chunks[TOK:]
+    block_ref[...] = jnp.dot(order, normed, preferred_element_type=F32).astype(BF16)
 
 
 def project_kernel(grid_ref, owner_ref, wa_ref, wb_ref, *refs):
-    out_ref = refs[CHIPS]
+    own_ref, one_ref, two_ref, three_ref, four_ref, out_ref = refs
+    chunks = [(own_ref, 0), (one_ref, 0), (one_ref, TOK), (two_ref, 0), (two_ref, TOK)]
+    chunks += [(three_ref, 0), (three_ref, TOK), (four_ref, 0)]
     halves = []
     for w_ref in (wa_ref, wb_ref):
         part = 0.0
         for corner in range(4):
             rows = jnp.concatenate(
-                [b[16 * corner : 16 * corner + 16, :] for b in refs[:CHIPS]], axis=0
+                [ref[pl.ds(at + 16 * corner, 16), :] for ref, at in chunks], axis=0
             )
             part = part + jnp.dot(
                 rows, w_ref[D * corner : D * corner + D, :], preferred_element_type=F32
@@ -310,10 +310,10 @@
     head_out = call(
         attention_kernel,
         shape((CHIPS, 2, HD // 2, 128), BF16),
-        [SM, VM],
+        [VM],
         flops=1 << 29,
         bytes_accessed=1 << 20,
-    )(grid_sizes, heads_all.reshape(SEQ, 256))
+    )(heads_all.reshape(SEQ, 256))
     groups = [[2 * c + p for c in range(CHIPS)] for p in range(2)]
     attended = lax.all_to_all(
         head_out,
@@ -331,9 +331,9 @@
         bytes_accessed=3 << 20,
     )(attended, hidden, *weight)
     recv = chip_shift(mixed, 0, 1)
-    normed, first, second = call(
+    normed, block = call(
         norm_kernel,
-        (shape((1, TOK, D), BF16), shape((TOK, D), BF16), shape((TOK, D), BF16)),
+        (shape((1, TOK, D), BF16), shape((128, D), BF16)),
         [VM] * 4,
         scratch=[pltpu.VMEM((128, D), BF16)],
         flops=1 << 22,
@@ -346,15 +346,13 @@
     def send(value, places):
         return two_way("seq", value, move, 16, places)
 
-    first1, second1 = send(first, 1), send(second, 1)
-    first2, second2 = send(first, 2), send(second, 2)
-    first3, second3 = send(first1, 2), send(second1, 2)
-    first4 = send(first2, 2)
-    chunks = [first, first1, second1, first2, second2, first3, second3, first4]
+    one, two = send(block, 1), send(block, 2)
+    three, four = send(one, 2), send(one[:TOK], 3)
+    chunks = [block, one, two, three, four]
     stats = call(
         project_kernel,
         shape((16, 128), F32),
-        [SM, SM] + [VM] * (2 + CHIPS),
+        [SM, SM] + [VM] * 7,
         flops=1 << 29,
         bytes_accessed=7 << 20,
         mib=16,

time: 126 us -> 124 us (0.984)
  starting transfers between devices: 70.3 us -> 62.3 us
  waiting for transfers between devices: 24.7 us -> 31.3 us
    ppermute x2, starting transfers between devices: 15.3 us -> 8.26 us  [chip_shift(): return lax.ppermute(x, 'seq', pairs)]
    ppermute x10 -> x7, waiting for transfers between devices: 14.6 us -> 21.2 us  [two_way(): return lax.ppermute(value, axes, pairs)]
    ppermute x10 -> x7, starting transfers between devices: 28.1 us -> 26.1 us  [two_way(): return lax.ppermute(value, axes, pairs)]
  transfers between devices with their start and end apart: 17 -> 14, of which waited for: 7 -> 6; matrix products, arithmetic and copies ran while one was open for 1% -> 2% of each run, Pallas kernels for 8% -> 7%
where the time goes in v3:
time: 124 us; the launch traced here: 123 us
  starting transfers between devices  62.3 us (50%)
  waiting for transfers between devices  31.3 us (25%)
  blocking collectives  13.5 us (11%)
  Pallas kernels  13 us (10%)
  other arithmetic  1.86 us (2%)
    ppermute x7, starting transfers between devices, two_way(): return lax.ppermute(value, axes, pairs)  26.1 us
    ppermute x7, waiting for transfers between devices, two_way(): return lax.ppermute(value, axes, pairs)  21.2 us
    all_to_all x1, blocking collectives, body(): lax.all_to_all(stats, 'seq', split_axis=0, concat_axis=0, tiled=True)  13.5 us
    all_to_all x1, starting transfers between devices, body(): lax.all_to_all(packed, 'seq', split_axis=0, concat_axis=0, tiled=True)  10.9 us
    ppermute x3, starting transfers between devices, shift_x(): return lax.ppermute(bundle, 'rows', pairs)  9.94 us
    ppermute x2, starting transfers between devices, chip_shift(): return lax.ppermute(x, 'seq', pairs)  8.26 us
    all_to_all x1, starting transfers between devices, body(): lax.all_to_all(head_out, 'seq', split_axis=0, concat_axis=0, axis_index_g...  7.09 us
    all_to_all x1, waiting for transfers between devices, body(): lax.all_to_all(head_out, 'seq', split_axis=0, concat_axis=0, axis_index_g...  5.36 us
  transfers between devices with their start and end apart: 14, of which 6 were waited for; matrix products, arithmetic and copies ran while one was open for 2% of the time, Pallas kernels for 7%

profile of v3, /device:TPU:1, one launch (start us, length us, event | category | flops | bytes accessed | tf_op | source)
XLA Modules:
  0.0 122.9 jit_solution(6427998318166576781)
XLA Ops:
  0.6 11.5 %collective-permute-start = (bf16[40,1280]{1,0:T(8,128)(2,1)}, bf16[40,1280]{1,0:T(8,128)(2,1)S(1)}, u32[]{:S(2)}, u32[]{:S(2)}) collective-permute-start(bf16[40,1280]{1,0:T(8,128)(2,1)} %param.15), channel_id=1, source_target_pairs={{0,64},{1,449},{2,66},{3,451},{4,68},{5,453},{6,70},{7,455},{8,72}... | collective-permute-start | bytes 307208 | tf_op jit(solution)/shard_map/ppermute | solution.py:261
  12.8 3.7 %shard_map.112 = bf16[16,64,256]{2,1,0:T(8,128)(2,1)} custom-call(s32[1,2,4]{2,1,0:T(2,128)} %bitcast.9, s32[1,64]{1,0:T(1,128)} %keep_ref.1, bf16[1,64,3840]{2,1,0:T(8,128)(2,1)} %qkv_ref.1), custom_call_target="tpu_custom_call" | custom-call | flops 4194304 | bytes 1048576 | tf_op jit(solution)/shard_map/pallas_call | solution.py:300
  16.5 10.9 %all-to-all-start = ((bf16[16,64,256]{2,1,0:T(8,128)(2,1)}), bf16[16,64,256]{2,1,0:T(8,128)(2,1)S(1)}, u32[]{:S(2)}, u32[]{:S(2)}) async-start(bf16[16,64,256]{2,1,0:T(8,128)(2,1)} %shard_map.112), calls=%async_computation | async-start | bytes 1048576 | tf_op jit(solution)/shard_map/all_to_all | solution.py:308
  27.4 2.0 %collective-permute-start.7 = (bf16[5120,256]{1,0:T(8,128)(2,1)}, bf16[5120,256]{1,0:T(8,128)(2,1)}, u32[]{:S(2)}, u32[]{:S(2)}) collective-permute-start(bf16[5120,256]{1,0:T(8,128)(2,1)} %wa_ref.1), channel_id=1, source_target_pairs={{0,1},{1,0},{2,3},{3,2},{4,5},{5,4},{6,7},{7,6},{8,9},{9,8},{10,11... | collective-permute-start | bytes 7864328 | tf_op jit(solution)/shard_map/ppermute | solution.py:252
  30.4 1.9 %collective-permute-start.1 = (bf16[80,1280]{1,0:T(8,128)(2,1)S(1)}, bf16[80,1280]{1,0:T(8,128)(2,1)S(1)}, u32[]{:S(2)}, u32[]{:S(2)}) collective-permute-start(bf16[80,1280]{1,0:T(8,128)(2,1)S(1)} %pad_maximum_fusion.1), channel_id=1, source_target_pairs={{0,128},{1,385},{2,130},{3,387},{4,132},{5,389},{6,134},{7,391},{8... | collective-permute-start | bytes 614408 | tf_op jit(solution)/shard_map/ppermute | solution.py:261
  33.2 7.0 %collective-permute-done.1 = bf16[80,1280]{1,0:T(8,128)(2,1)S(1)} collective-permute-done((bf16[80,1280]{1,0:T(8,128)(2,1)S(1)}, bf16[80,1280]{1,0:T(8,128)(2,1)S(1)}, u32[]{:S(2)}, u32[]{:S(2)}) %collective-permute-start.1) | collective-permute-done | bytes 204832 | tf_op jit(solution)/shard_map/ppermute | solution.py:261
  40.3 4.7 %collective-permute-start.5 = (bf16[160,1280]{1,0:T(8,128)(2,1)S(1)}, bf16[160,1280]{1,0:T(8,128)(2,1)}, u32[]{:S(2)}, u32[]{:S(2)}) collective-permute-start(bf16[160,1280]{1,0:T(8,128)(2,1)S(1)} %pad_maximum_fusion.own_ref), channel_id=1, source_target_pairs={{0,32},{16,48},{32,0},{48,16},{64,96},{80,112},{96,64},{112,80},{1... | collective-permute-start | bytes 1228808 | tf_op jit(solution)/shard_map/ppermute | solution.py:280
  45.0 2.8 %collective-permute-start.4 = (bf16[160,1280]{1,0:T(8,128)(2,1)S(1)}, bf16[160,1280]{1,0:T(8,128)(2,1)}, u32[]{:S(2)}, u32[]{:S(2)}) collective-permute-start(bf16[160,1280]{1,0:T(8,128)(2,1)S(1)} %pad_maximum_fusion.own_ref), channel_id=1, source_target_pairs={{0,48},{16,0},{32,16},{48,32},{64,112},{80,64},{96,80},{112,96},{1... | collective-permute-start | bytes 1228808 | tf_op jit(solution)/shard_map/ppermute | solution.py:280
  47.7 2.5 %collective-permute-start.3 = (bf16[160,1280]{1,0:T(8,128)(2,1)S(1)}, bf16[160,1280]{1,0:T(8,128)(2,1)}, u32[]{:S(2)}, u32[]{:S(2)}) collective-permute-start(bf16[160,1280]{1,0:T(8,128)(2,1)S(1)} %pad_maximum_fusion.own_ref), channel_id=1, source_target_pairs={{0,16},{16,32},{32,48},{48,0},{64,80},{80,96},{96,112},{112,64},{1... | collective-permute-start | bytes 1228808 | tf_op jit(solution)/shard_map/ppermute | solution.py:280
  50.3 2.6 %shard_map.113 = bf16[8,2,40,128]{3,2,1,0:T(8,128)(2,1)} custom-call(bf16[1024,256]{1,0:T(8,128)(2,1)S(1)} %bitcast.6), custom_call_target="tpu_custom_call" | custom-call | flops 536870912 | bytes 1048576 | tf_op jit(solution)/shard_map/pallas_call | solution.py:310
  52.9 7.1 %all-to-all-start.1 = ((bf16[8,2,40,128]{3,2,1,0:T(8,128)(2,1)}), bf16[8,2,40,128]{3,2,1,0:T(8,128)(2,1)S(1)}, u32[]{:S(2)}, u32[]{:S(2)}) async-start(bf16[8,2,40,128]{3,2,1,0:T(8,128)(2,1)} %shard_map.113), calls=%async_computation.1 | async-start | bytes 327680 | tf_op jit(solution)/shard_map/all_to_all | solution.py:318
  60.0 3.0 %collective-permute-done.4.minus_ref = bf16[160,1280]{1,0:T(8,128)(2,1)} collective-permute-done((bf16[160,1280]{1,0:T(8,128)(2,1)S(1)}, bf16[160,1280]{1,0:T(8,128)(2,1)}, u32[]{:S(2)}, u32[]{:S(2)}) %collective-permute-start.4) | collective-permute-done | bytes 409632 | tf_op jit(solution)/shard_map/ppermute | solution.py:280
  63.0 5.4 %all-to-all-done.1.heads_ref = bf16[8,2,40,128]{3,2,1,0:T(8,128)(2,1)S(1)} async-done(((bf16[8,2,40,128]{3,2,1,0:T(8,128)(2,1)}), bf16[8,2,40,128]{3,2,1,0:T(8,128)(2,1)S(1)}, u32[]{:S(2)}, u32[]{:S(2)}) %all-to-all-start.1) | async-done | bytes 163872 | tf_op jit(solution)/shard_map/all_to_all | solution.py:318
  68.3 1.8 %shard_map.114.own_ref = f32[128,1280]{1,0:T(8,128)S(1)} custom-call(bf16[8,2,40,128]{3,2,1,0:T(8,128)(2,1)S(1)} %all-to-all-done.1.heads_ref, bf16[1,64,1280]{2,1,0:T(8,128)(2,1)S(1)} %copy-done.1, bf16[160,1280]{1,0:T(8,128)(2,1)S(1)} %pad_maximum_fusion.own_ref, bf16[160,1280]{1,0:T(8,128)(2,1)} %collective-permute-done.3.plus_ref, ...), custom_call_target="tpu_custom_call" | custom-call | flops 268435456 | bytes 3145728 | tf_op jit(solution)/shard_map/pallas_call | solution.py:326
  70.1 6.2 %collective-permute-start.6 = (f32[128,1280]{1,0:T(8,128)S(1)}, f32[128,1280]{1,0:T(8,128)S(1)}, u32[]{:S(2)}, u32[]{:S(2)}) collective-permute-start(f32[128,1280]{1,0:T(8,128)S(1)} %shard_map.114.own_ref), channel_id=1, source_target_pairs={{0,1},{1,0},{2,3},{3,2},{4,5},{5,4},{6,7},{7,6},{8,9},{9,8},{10,11... | collective-permute-start | bytes 1966088 | tf_op jit(solution)/shard_map/ppermute | solution.py:252
  76.4 1.7 %collective-permute-done.6.recv_ref = f32[128,1280]{1,0:T(8,128)S(1)} collective-permute-done((f32[128,1280]{1,0:T(8,128)S(1)}, f32[128,1280]{1,0:T(8,128)S(1)}, u32[]{:S(2)}, u32[]{:S(2)}) %collective-permute-start.6) | collective-permute-done | bytes 655392 | tf_op jit(solution)/shard_map/ppermute | solution.py:252
  79.1 1.9 %collective-permute-start.8 = (bf16[128,1280]{1,0:T(8,128)(2,1)S(1)}, bf16[128,1280]{1,0:T(8,128)(2,1)S(1)}, u32[]{:S(2)}, u32[]{:S(2)}) collective-permute-start(bf16[128,1280]{1,0:T(8,128)(2,1)S(1)} %get-tuple-element.8.refs_0_), channel_id=1, source_target_pairs={{0,2},{1,15},{2,4},{3,1},{4,6},{5,3},{6,8},{7,5},{8,10},{9,7},{10,... | collective-permute-start | bytes 983048 | tf_op jit(solution)/shard_map/ppermute | solution.py:261
  81.0 2.0 %collective-permute-start.9 = (bf16[128,1280]{1,0:T(8,128)(2,1)S(1)}, bf16[128,1280]{1,0:T(8,128)(2,1)S(1)}, u32[]{:S(2)}, u32[]{:S(2)}) collective-permute-start(bf16[128,1280]{1,0:T(8,128)(2,1)S(1)} %get-tuple-element.8.refs_0_), channel_id=1, source_target_pairs={{0,4},{1,13},{2,6},{3,15},{4,8},{5,1},{6,10},{7,3},{8,12},{9,5},{1... | collective-permute-start | bytes 983048 | tf_op jit(solution)/shard_map/ppermute | solution.py:261
  83.1 4.2 %collective-permute-done.8.refs_1_ = bf16[128,1280]{1,0:T(8,128)(2,1)S(1)} collective-permute-done((bf16[128,1280]{1,0:T(8,128)(2,1)S(1)}, bf16[128,1280]{1,0:T(8,128)(2,1)S(1)}, u32[]{:S(2)}, u32[]{:S(2)}) %collective-permute-start.8) | collective-permute-done | bytes 327712 | tf_op jit(solution)/shard_map/ppermute | solution.py:261
  87.2 2.0 %collective-permute-start.10 = (bf16[128,1280]{1,0:T(8,128)(2,1)S(1)}, bf16[128,1280]{1,0:T(8,128)(2,1)S(1)}, u32[]{:S(2)}, u32[]{:S(2)}) collective-permute-start(bf16[128,1280]{1,0:T(8,128)(2,1)S(1)} %collective-permute-done.8.refs_1_), channel_id=1, source_target_pairs={{0,4},{1,13},{2,6},{3,15},{4,8},{5,1},{6,10},{7,3},{8,12},{9,5},{1... | collective-permute-start | bytes 983048 | tf_op jit(solution)/shard_map/ppermute | solution.py:261
  89.2 6.1 %collective-permute-start.11 = (bf16[64,1280]{1,0:T(8,128)(2,1)S(1)}, bf16[64,1280]{1,0:T(8,128)(2,1)S(1)}, u32[]{:S(2)}, u32[]{:S(2)}) collective-permute-start(bf16[64,1280]{1,0:T(8,128)(2,1)S(1)} %slice.4), channel_id=1, source_target_pairs={{0,6},{1,11},{2,8},{3,13},{4,10},{5,15},{6,12},{7,1},{8,14},{9,3},... | collective-permute-start | bytes 491528 | tf_op jit(solution)/shard_map/ppermute | solution.py:261
  95.4 10.0 %collective-permute-done.11.refs_4_ = bf16[64,1280]{1,0:T(8,128)(2,1)S(1)} collective-permute-done((bf16[64,1280]{1,0:T(8,128)(2,1)S(1)}, bf16[64,1280]{1,0:T(8,128)(2,1)S(1)}, u32[]{:S(2)}, u32[]{:S(2)}) %collective-permute-start.11) | collective-permute-done | bytes 163872 | tf_op jit(solution)/shard_map/ppermute | solution.py:261
  105.4 2.8 %shard_map.116 = f32[16,128]{1,0:T(8,128)S(1)} custom-call(s32[1,2,4]{2,1,0:T(2,128)S(1)} %bitcast.10, s32[1,4]{1,0:T(1,128)S(1)} %copy-done.5, bf16[5120,256]{1,0:T(8,128)(2,1)S(1)} %copy-done, bf16[5120,256]{1,0:T(8,128)(2,1)} %collective-permute-done.7.wb_ref, bf16[128,1280]{1,0:T(8,128)(2,1)S(1)} %get-tuple-element.8.refs_0_, ...), custom_call_target="tpu_custom_call" | custom-call | flops 536870912 | bytes 7340032 | tf_op jit(solution)/shard_map/pallas_call | solution.py:352
  108.2 13.5 %all_to_all.21 = f32[16,1,128]{2,1,0:T(1,128)S(1)} all-to-all(f32[16,1,128]{2,1,0:T(1,128)S(1)} %bitcast.7), channel_id=1, replica_groups=mesh['rows'=32,'seq'=16] {'seq'}, dimensions={0} | all-to-all | bytes 16384 | tf_op jit(solution)/shard_map/all_to_all | solution.py:360
  (27 shorter events, 4.8 us)
Async XLA Ops:
  0.6 28.8 %collective-permute-start = (bf16[40,1280]{1,0:T(8,128)(2,1)}, bf16[40,1280]{1,0:T(8,128)(2,1)S(1)}, u32[]{:S(2)}, u32[]{:S(2)}) collective-permute-start(bf16[40,1280]{1,0:T(8,128)(2,1)} %param.15), channel_id=1, source_target_pairs={{0,64},{1,449},{2,66},{3,451},{4,68},{5,453},{6,70},{7,455},{8,72}... | collective-permute-start | bytes 307208 | tf_op jit(solution)/shard_map/ppermute | solution.py:261
  12.1 20.2 %collective-permute-start.2 = (bf16[40,1280]{1,0:T(8,128)(2,1)}, bf16[40,1280]{1,0:T(8,128)(2,1)S(1)}, u32[]{:S(2)}, u32[]{:S(2)}) collective-permute-start(bf16[40,1280]{1,0:T(8,128)(2,1)} %param.15), channel_id=1, source_target_pairs={{0,256},{2,258},{4,260},{6,262},{8,264},{10,266},{12,268},{14,270}... | collective-permute-start | bytes 307208 | tf_op jit(solution)/shard_map/ppermute | solution.py:261
  16.5 51.8 %copy-start.1 = (bf16[1,64,1280]{2,1,0:T(8,128)(2,1)S(1)}, bf16[1,64,1280]{2,1,0:T(8,128)(2,1)}, u32[]{:S(2)}) copy-start(bf16[1,64,1280]{2,1,0:T(8,128)(2,1)} %hidden_ref.1) | copy-start | bytes 491524
  16.5 33.7 %all-to-all-start = ((bf16[16,64,256]{2,1,0:T(8,128)(2,1)}), bf16[16,64,256]{2,1,0:T(8,128)(2,1)S(1)}, u32[]{:S(2)}, u32[]{:S(2)}) async-start(bf16[16,64,256]{2,1,0:T(8,128)(2,1)} %shard_map.112), calls=%async_computation | async-start | bytes 1048576 | tf_op jit(solution)/shard_map/all_to_all | solution.py:308
  27.4 78.0 %collective-permute-start.7 = (bf16[5120,256]{1,0:T(8,128)(2,1)}, bf16[5120,256]{1,0:T(8,128)(2,1)}, u32[]{:S(2)}, u32[]{:S(2)}) collective-permute-start(bf16[5120,256]{1,0:T(8,128)(2,1)} %wa_ref.1), channel_id=1, source_target_pairs={{0,1},{1,0},{2,3},{3,2},{4,5},{5,4},{6,7},{7,6},{8,9},{9,8},{10,11... | collective-permute-start | bytes 7864328 | tf_op jit(solution)/shard_map/ppermute | solution.py:252
  30.4 9.9 %collective-permute-start.1 = (bf16[80,1280]{1,0:T(8,128)(2,1)S(1)}, bf16[80,1280]{1,0:T(8,128)(2,1)S(1)}, u32[]{:S(2)}, u32[]{:S(2)}) collective-permute-start(bf16[80,1280]{1,0:T(8,128)(2,1)S(1)} %pad_maximum_fusion.1), channel_id=1, source_target_pairs={{0,128},{1,385},{2,130},{3,387},{4,132},{5,389},{6,134},{7,391},{8... | collective-permute-start | bytes 614408 | tf_op jit(solution)/shard_map/ppermute | solution.py:261
  40.3 37.8 %copy-start.3 = (f32[1280]{0:T(1024)S(1)}, f32[1280]{0:T(1024)}, u32[]{:S(2)}) copy-start(f32[1280]{0:T(1024)} %gain_ref.1) | copy-start | bytes 15364
  40.3 37.8 %copy-start.4 = (f32[1280]{0:T(1024)S(1)}, f32[1280]{0:T(1024)}, u32[]{:S(2)}) copy-start(f32[1280]{0:T(1024)} %bias_ref.1) | copy-start | bytes 15364
  40.3 19.7 %collective-permute-start.5 = (bf16[160,1280]{1,0:T(8,128)(2,1)S(1)}, bf16[160,1280]{1,0:T(8,128)(2,1)}, u32[]{:S(2)}, u32[]{:S(2)}) collective-permute-start(bf16[160,1280]{1,0:T(8,128)(2,1)S(1)} %pad_maximum_fusion.own_ref), channel_id=1, source_target_pairs={{0,32},{16,48},{32,0},{48,16},{64,96},{80,112},{96,64},{112,80},{1... | collective-permute-start | bytes 1228808 | tf_op jit(solution)/shard_map/ppermute | solution.py:280
  45.0 18.0 %collective-permute-start.4 = (bf16[160,1280]{1,0:T(8,128)(2,1)S(1)}, bf16[160,1280]{1,0:T(8,128)(2,1)}, u32[]{:S(2)}, u32[]{:S(2)}) collective-permute-start(bf16[160,1280]{1,0:T(8,128)(2,1)S(1)} %pad_maximum_fusion.own_ref), channel_id=1, source_target_pairs={{0,48},{16,0},{32,16},{48,32},{64,112},{80,64},{96,80},{112,96},{1... | collective-permute-start | bytes 1228808 | tf_op jit(solution)/shard_map/ppermute | solution.py:280
  47.7 15.2 %collective-permute-start.3 = (bf16[160,1280]{1,0:T(8,128)(2,1)S(1)}, bf16[160,1280]{1,0:T(8,128)(2,1)}, u32[]{:S(2)}, u32[]{:S(2)}) collective-permute-start(bf16[160,1280]{1,0:T(8,128)(2,1)S(1)} %pad_maximum_fusion.own_ref), channel_id=1, source_target_pairs={{0,16},{16,32},{32,48},{48,0},{64,80},{80,96},{96,112},{112,64},{1... | collective-permute-start | bytes 1228808 | tf_op jit(solution)/shard_map/ppermute | solution.py:280
  52.9 52.6 %copy-start = (bf16[5120,256]{1,0:T(8,128)(2,1)S(1)}, bf16[5120,256]{1,0:T(8,128)(2,1)}, u32[]{:S(2)}) copy-start(bf16[5120,256]{1,0:T(8,128)(2,1)} %wa_ref.1) | copy-start | bytes 7864324
  52.9 52.6 %copy-start.2 = (s32[1,4,2]{1,2,0:T(2,128)S(1)}, s32[1,4,2]{1,2,0:T(2,128)}, u32[]{:S(2)}) copy-start(s32[1,4,2]{1,2,0:T(2,128)} %param.13) | copy-start | bytes 100
  52.9 52.6 %copy-start.5 = (s32[1,4]{1,0:T(1,128)S(1)}, s32[1,4]{1,0:T(1,128)}, u32[]{:S(2)}) copy-start(s32[1,4]{1,0:T(1,128)} %owner_ref.3) | copy-start | bytes 52
  52.9 15.5 %all-to-all-start.1 = ((bf16[8,2,40,128]{3,2,1,0:T(8,128)(2,1)}), bf16[8,2,40,128]{3,2,1,0:T(8,128)(2,1)S(1)}, u32[]{:S(2)}, u32[]{:S(2)}) async-start(bf16[8,2,40,128]{3,2,1,0:T(8,128)(2,1)} %shard_map.113), calls=%async_computation.1 | async-start | bytes 327680 | tf_op jit(solution)/shard_map/all_to_all | solution.py:318
  70.1 8.0 %collective-permute-start.6 = (f32[128,1280]{1,0:T(8,128)S(1)}, f32[128,1280]{1,0:T(8,128)S(1)}, u32[]{:S(2)}, u32[]{:S(2)}) collective-permute-start(f32[128,1280]{1,0:T(8,128)S(1)} %shard_map.114.own_ref), channel_id=1, source_target_pairs={{0,1},{1,0},{2,3},{3,2},{4,5},{5,4},{6,7},{7,6},{8,9},{9,8},{10,11... | collective-permute-start | bytes 1966088 | tf_op jit(solution)/shard_map/ppermute | solution.py:252
  79.1 8.1 %collective-permute-start.8 = (bf16[128,1280]{1,0:T(8,128)(2,1)S(1)}, bf16[128,1280]{1,0:T(8,128)(2,1)S(1)}, u32[]{:S(2)}, u32[]{:S(2)}) collective-permute-start(bf16[128,1280]{1,0:T(8,128)(2,1)S(1)} %get-tuple-element.8.refs_0_), channel_id=1, source_target_pairs={{0,2},{1,15},{2,4},{3,1},{4,6},{5,3},{6,8},{7,5},{8,10},{9,7},{10,... | collective-permute-start | bytes 983048 | tf_op jit(solution)/shard_map/ppermute | solution.py:261
  81.0 14.3 %collective-permute-start.9 = (bf16[128,1280]{1,0:T(8,128)(2,1)S(1)}, bf16[128,1280]{1,0:T(8,128)(2,1)S(1)}, u32[]{:S(2)}, u32[]{:S(2)}) collective-permute-start(bf16[128,1280]{1,0:T(8,128)(2,1)S(1)} %get-tuple-element.8.refs_0_), channel_id=1, source_target_pairs={{0,4},{1,13},{2,6},{3,15},{4,8},{5,1},{6,10},{7,3},{8,12},{9,5},{1... | collective-permute-start | bytes 983048 | tf_op jit(solution)/shard_map/ppermute | solution.py:261
  87.2 18.2 %collective-permute-start.10 = (bf16[128,1280]{1,0:T(8,128)(2,1)S(1)}, bf16[128,1280]{1,0:T(8,128)(2,1)S(1)}, u32[]{:S(2)}, u32[]{:S(2)}) collective-permute-start(bf16[128,1280]{1,0:T(8,128)(2,1)S(1)} %collective-permute-done.8.refs_1_), channel_id=1, source_target_pairs={{0,4},{1,13},{2,6},{3,15},{4,8},{5,1},{6,10},{7,3},{8,12},{9,5},{1... | collective-permute-start | bytes 983048 | tf_op jit(solution)/shard_map/ppermute | solution.py:261
  89.2 16.2 %collective-permute-start.11 = (bf16[64,1280]{1,0:T(8,128)(2,1)S(1)}, bf16[64,1280]{1,0:T(8,128)(2,1)S(1)}, u32[]{:S(2)}, u32[]{:S(2)}) collective-permute-start(bf16[64,1280]{1,0:T(8,128)(2,1)S(1)} %slice.4), channel_id=1, source_target_pairs={{0,6},{1,11},{2,8},{3,13},{4,10},{5,15},{6,12},{7,1},{8,14},{9,3},... | collective-permute-start | bytes 491528 | tf_op jit(solution)/shard_map/ppermute | solution.py:261
